TPU v7x, 256 devices: a whole 4x4x8 slice. The times are simulated.
256 devices in a mesh: coil: 32 (over z, y), slab: 8 (over x, core).
Axes of the slice: x: 4, y: 4, z: 8, core: 2. Of those that a mesh axis runs over, the one named last changes fastest.
Arguments:
- cotangent: float32 [32, 2, 256, 256], P('coil', None, 'slab'), may hold values from -60 to 60
- saved_solution: float32 [32, 2, 256, 256], P('coil', None, 'slab'), may hold values from -6 to 6
- coil_maps: bfloat16 [32, 32, 2, 256, 256], P('coil', None, None, 'slab'), may hold values from -1.5 to 1.5
- kspace: bfloat16 [32, 32, 2, 256, 256], P('coil', None, None, 'slab'), may hold values from -6 to 6
- mask_logit: float32 [32, 256], P(None, 'slab'), may hold values from -4.5 to 4.5
- reach: int32 [32, 256], P(None, 'slab'), may hold values from 0 to 256, as said below
Outputs:
- image_grad: float32 [32, 2, 256, 256], P('coil', None, 'slab')
- kspace_grad: bfloat16 [32, 32, 2, 256, 256], P('coil', None, None, 'slab')
- logit_grad: float32 [32, 256], P(None, 'slab')
Inputs may be any that keep to these rules, and one draw needn't show every extreme that they name: reach[z, y] is 0 (line not acquired) or between 128 and 256; line [0, 0] is always fully acquired and line [0, 128] never.
All inputs are finite; a program needn't handle non-finite values.
Results may differ from a plain program's by a relative error of at most 0.02.
Values may be sent and summed in bfloat16 or wider, within the bound.
A program may use at most 64 MiB of HBM per device.

v0:
```python
import math

import jax
import jax.numpy as jnp
from jax import lax
from jax.sharding import PartitionSpec as P

NX = 256
NY = 256
NZ = 32
ITERS = 2


DAMPING = 0.2


def dft_table(length, sign):
    index = jnp.arange(length, dtype=jnp.int32)
    phase = (index[:, None] * index[None, :] % length).astype(jnp.float32) * (
        2.0 * math.pi / length
    )
    factor = 1.0 / math.sqrt(length)
    cosine = jnp.cos(phase) * factor
    sine = sign * jnp.sin(phase) * factor
    table = jnp.stack(
        [jnp.stack([cosine, sine], axis=1), jnp.stack([-sine, cosine], axis=1)], axis=0
    )
    return table.astype(jnp.bfloat16)


def complex_product(factor, operand):
    factor_re, factor_im = (factor[:, 0], factor[:, 1])
    operand_re, operand_im = (operand[:, 0], operand[:, 1])
    return jnp.stack(
        [
            factor_re * operand_re - factor_im * operand_im,
            factor_re * operand_im + factor_im * operand_re,
        ],
        axis=1,
    )


def conjugate_product(factor, operand):
    factor_re, factor_im = (factor[:, 0], factor[:, 1])
    operand_re, operand_im = (operand[:, 0], operand[:, 1])
    return jnp.stack(
        [
            factor_re * operand_re + factor_im * operand_im,
            factor_re * operand_im - factor_im * operand_re,
        ],
        axis=1,
    )


def shards(cotangent, saved_solution, coil_maps, kspace, mask_logit, reach):
    y_fwd, y_inv = (dft_table(NY, -1.0), dft_table(NY, 1.0))
    z_fwd, z_inv = (dft_table(NZ, -1.0), dft_table(NZ, 1.0))
    x_fwd, x_inv = (dft_table(NX, -1.0), dft_table(NX, 1.0))
    maps = coil_maps[0]
    data = kspace[0].astype(jnp.float32)
    readout = jnp.arange(NX, dtype=jnp.int32)
    centred = (readout + NX // 2) % NX
    sampled = (centred[None, None, :] >= (NX - reach)[:, :, None]).astype(jnp.float32)
    gate = jax.nn.sigmoid(mask_logit)
    weight = sampled * gate[:, :, None]
    squared = (weight * weight)[:, None]

    def front(piece):
        product = complex_product(maps.astype(jnp.float32), piece.astype(jnp.float32)).astype(
            jnp.bfloat16
        )
        return jnp.einsum(
            "zixn,inok->zoxk", product, y_fwd, preferred_element_type=jnp.float32
        ).astype(jnp.bfloat16)

    def gathered_front(shard):
        return front(lax.all_gather(shard, "coil", axis=0, tiled=True))

    def to_kspace(rows):
        mixed = jnp.einsum(
            "nixk,inom->moxk", rows, z_fwd, preferred_element_type=jnp.float32
        ).astype(jnp.bfloat16)
        swapped = lax.all_to_all(mixed, "slab", split_axis=3, concat_axis=2, tiled=True)
        return jnp.einsum("zink,inoq->zokq", swapped, x_fwd, preferred_element_type=jnp.float32)

    residual = cotangent

    def inner_norm(values):
        return lax.psum(jnp.sum(values * values), ("coil", "slab"))

    direction = residual
    solution = jnp.zeros(residual.shape, jnp.float32)
    norm_now = inner_norm(residual)
    for step in range(ITERS):
        apply_rows = gathered_front(direction.astype(jnp.bfloat16))
        apply_spectrum = (squared * to_kspace(apply_rows)).astype(jnp.bfloat16)
        to_mixed = jnp.einsum(
            "zikq,iqon->zonk", apply_spectrum, x_inv, preferred_element_type=jnp.float32
        ).astype(jnp.bfloat16)
        to_swapped = lax.all_to_all(to_mixed, "slab", split_axis=2, concat_axis=3, tiled=True)
        apply_image_rows = jnp.einsum(
            "mixk,imon->noxk", to_swapped, z_inv, preferred_element_type=jnp.float32
        ).astype(jnp.bfloat16)
        image = jnp.einsum(
            "zixk,ikon->zoxn", apply_image_rows, y_inv, preferred_element_type=jnp.float32
        )
        summed = lax.psum_scatter(
            conjugate_product(maps.astype(jnp.float32), image).astype(jnp.bfloat16),
            "coil",
            scatter_dimension=0,
            tiled=True,
        ).astype(jnp.float32)
        image = summed + DAMPING * direction
        alpha = norm_now / lax.psum(jnp.sum(direction * image), ("coil", "slab"))
        solution = solution + alpha * direction
        if step + 1 < ITERS:
            residual = residual - alpha * image
            norm_next = inner_norm(residual)
            direction = residual + norm_next / norm_now * direction
            norm_now = norm_next
    image_grad = DAMPING * solution
    solution_rows = gathered_front(solution.astype(jnp.bfloat16))
    saved_rows = gathered_front(saved_solution.astype(jnp.bfloat16))
    solution_k = to_kspace(solution_rows)
    saved_k = to_kspace(saved_rows)
    kspace_grad = (weight[:, None] * solution_k).astype(jnp.bfloat16)[None]
    value = solution_k[:, 0] * (data[:, 0] - 2.0 * weight * saved_k[:, 0]) + solution_k[:, 1] * (
        data[:, 1] - 2.0 * weight * saved_k[:, 1]
    )
    partial_grad = gate * (1.0 - gate) * jnp.sum(sampled * value, axis=2)
    logit_grad = lax.psum(partial_grad, "coil")
    return (image_grad, kspace_grad, logit_grad)


def solution(mesh):
    placed = (
        P("coil", None, "slab", None),
        P("coil", None, "slab", None),
        P("coil", None, None, "slab", None),
        P("coil", None, None, "slab", None),
        P(None, "slab"),
        P(None, "slab"),
    )
    return jax.shard_map(
        shards,
        mesh=mesh,
        in_specs=placed,
        out_specs=(
            P("coil", None, "slab", None),
            P("coil", None, None, "slab", None),
            P(None, "slab"),
        ),
        check_vma=False,
    )
```

profile of v0, /device:TPU:2, one launch (start us, length us, event | category | flops | bytes accessed | tf_op | source)
XLA Modules:
  0.0 1217.0 jit_solution(4830833247057705554)
XLA Ops:
  7.2 2.1 fusion.113
  14.3 1.8 bitcast_convert_fusion.13
  17.1 73.5 %all-gather.5.cloned.1.call-done = bf16[32,2,32,256]{3,2,1,0:T(8,128)(2,1)} async-done(((bf16[1,2,32,256]{3,2,1,0:T(8,128)(2,1)}), bf16[32,2,32,256]{3,2,1,0:T(8,128)(2,1)}) %all-gather.5.cloned.1.call-update) | async-done | bytes 1048592 | tf_op jit(solution)/shard_map/all_gather | solution.py:77
  93.9 2.3 fusion.2
  96.3 6.5 copy.95
  102.8 7.8 reshape.284
  110.6 5.5 all-to-all-start
  116.1 2.0 pad_maximum_fusion.2
  119.5 11.0 all-to-all-done
  130.6 4.5 reshape.285
  135.1 6.7 copy.96
  141.8 5.4 reshape.236
  147.2 3.7 fusion.11
  150.9 7.2 copy.98
  158.1 7.8 reshape.286
  165.9 4.9 all-to-all-start.1
  171.1 3.2 copy_convert_fusion
  174.2 11.1 all-to-all-done.1
  185.4 4.5 reshape.287
  189.9 6.9 copy.221
  196.8 5.3 all_to_all.85
  204.8 1.8 subtract_convert_fusion
  209.0 146.7 %all-reduce.6.cloned.1.call-done = bf16[32,2,32,256]{3,2,0,1:T(8,128)(2,1)} async-done(((bf16[32,2,32,256]{3,2,0,1:T(8,128)(2,1)}), bf16[32,2,32,256]{3,2,0,1:T(8,128)(2,1)}) %all-reduce.6.cloned.1.call-update) | async-done | bytes 1048592
  355.6 1.9 fusion.85
  357.5 72.7 %all-reduce.2 = (f32[]{:T(128)}, f32[]{:T(128)}) all-reduce(f32[]{:T(128)} %get-tuple-element.40, f32[]{:T(128)} %fusion.85), channel_id=1, replica_groups=mesh['coil'=32,'slab'=8] {'coil','slab'}, use_global_device_ids=true, to_apply=%region_1.2 | all-reduce | flops 2 | bytes 16 | tf_op jit(solution)/shard_map/psum | solution.py:89
  431.6 1.9 multiply_reduce_fusion.1
  433.5 73.5 %psum.37 = f32[]{:T(128)} all-reduce(f32[]{:T(128)} %multiply_reduce_fusion.1), channel_id=1, replica_groups=mesh['coil'=32,'slab'=8] {'coil','slab'}, use_global_device_ids=true, to_apply=%region_6.7 | all-reduce | flops 1 | bytes 8 | tf_op jit(solution)/shard_map/psum | solution.py:89
  508.2 1.9 convert_bitcast_fusion.1
  510.4 73.1 %all-gather.7.cloned.1.call-done = bf16[32,2,32,256]{3,2,1,0:T(8,128)(2,1)} async-done(((bf16[1,2,32,256]{3,2,1,0:T(8,128)(2,1)}), bf16[32,2,32,256]{3,2,1,0:T(8,128)(2,1)}) %all-gather.7.cloned.1.call-update) | async-done | bytes 1048592 | tf_op jit(solution)/shard_map/all_gather | solution.py:77
  586.9 2.3 fusion.4
  589.2 6.6 copy.113
  595.8 7.0 reshape.288
  602.8 19.3 %all_to_all.108 = bf16[8,2,32768]{2,1,0:T(2,128)(2,1)} all-to-all(bf16[8,2,32768]{2,1,0:T(2,128)(2,1)S(1)} %reshape.288), channel_id=1, replica_groups=mesh['coil'=32,'slab'=8] {'slab'}, dimensions={0} | all-to-all | bytes 2097152 | tf_op jit(solution)/shard_map/all_to_all | solution.py:83
  622.1 7.0 reshape.289
  629.1 6.7 copy.114
  635.8 5.3 reshape.251
  641.2 3.7 fusion.13
  644.9 7.3 copy.116
  652.2 7.0 reshape.290
  659.1 19.5 %all_to_all.109 = bf16[8,2,32768]{2,1,0:T(2,128)(2,1)} all-to-all(bf16[8,2,32768]{2,1,0:T(2,128)(2,1)S(1)} %reshape.290), channel_id=1, replica_groups=mesh['coil'=32,'slab'=8] {'slab'}, dimensions={0} | all-to-all | bytes 2097152 | tf_op jit(solution)/shard_map/all_to_all | solution.py:100
  678.7 7.0 reshape.291
  685.7 6.9 copy.220
  692.6 5.3 all_to_all.93
  702.0 147.1 %all-reduce.8.cloned.1.call-done = bf16[32,2,32,256]{3,2,0,1:T(8,128)(2,1)} async-done(((bf16[32,2,32,256]{3,2,0,1:T(8,128)(2,1)}), bf16[32,2,32,256]{3,2,0,1:T(8,128)(2,1)}) %all-reduce.8.cloned.1.call-update) | async-done | bytes 1048592
  849.1 2.0 multiply_reduce_fusion
  851.0 72.6 %psum.38 = f32[]{:T(128)} all-reduce(f32[]{:T(128)} %multiply_reduce_fusion), channel_id=1, replica_groups=mesh['coil'=32,'slab'=8] {'coil','slab'}, use_global_device_ids=true, to_apply=%region_9.10 | all-reduce | flops 1 | bytes 8 | tf_op jit(solution)/shard_map/psum | solution.py:114
  924.9 2.0 convert_bitcast_fusion
  926.9 2.3 fusion.7
  929.2 6.6 copy.130
  935.7 7.8 reshape.294
  943.6 5.8 all-to-all-start.5
  949.3 51.3 %all-gather.9.cloned.1.call-done = bf16[32,2,32,256]{3,2,1,0:T(8,128)(2,1)} async-done(((bf16[1,2,32,256]{3,2,1,0:T(8,128)(2,1)}), bf16[32,2,32,256]{3,2,1,0:T(8,128)(2,1)}) %all-gather.9.cloned.1.call-update) | async-done | bytes 1048592 | tf_op jit(solution)/shard_map/all_gather | solution.py:77
  1004.0 2.3 fusion.6
  1006.3 6.6 copy.126
  1012.9 7.8 reshape.292
  1020.7 4.8 all-to-all-start.4
  1027.0 4.5 reshape.295
  1031.5 6.7 copy.131
  1038.2 5.3 reshape.272
  1043.6 3.0 convolution_bitcast_fusion
  1046.6 7.0 reshape.293
  1053.6 6.7 copy.127
  1060.3 5.3 reshape.266
  1069.9 140.1 %psum.39 = f32[32,32]{1,0:T(8,128)} all-reduce(f32[32,32]{1,0:T(8,128)S(1)} %fusion.98), channel_id=1, replica_groups=mesh['coil'=32,'slab'=8] {'coil'}, use_global_device_ids=true, to_apply=%region_11.12 | all-reduce | flops 1024 | bytes 8192 | tf_op jit(solution)/shard_map/psum | solution.py:131
  (80 shorter events, 32.4 us)
Async XLA Ops:
  7.2 83.4 %all-gather.5.cloned.1.call-start = ((), (), s32[]{:S(2)}) async-start(), calls=%async_computation.6 | async-start | bytes 1081344 | tf_op jit(solution)/shard_map/all_gather | solution.py:77
  9.3 161.7 %all-gather.11.cloned.1.call-start = ((), (), s32[]{:S(2)}) async-start(), calls=%async_computation.9 | async-start | bytes 1081344 | tf_op jit(solution)/shard_map/all_gather | solution.py:77
  16.1 77.8 %copy-start.8 = (bf16[1,32,2,32]{1,3,0,2:T(8,128)(2,1)}, bf16[1,32,2,32]{1,3,0,2:T(8,128)(2,1)S(1)}, u32[]{:S(2)}) copy-start(bf16[1,32,2,32]{1,3,0,2:T(8,128)(2,1)S(1)} %get-tuple-element.44) | copy-start | bytes 12292
  16.1 77.8 %copy-start.10 = (bf16[1,32,2,32]{1,3,0,2:T(8,128)(2,1)}, bf16[1,32,2,32]{1,3,0,2:T(8,128)(2,1)S(1)}, u32[]{:S(2)}) copy-start(bf16[1,32,2,32]{1,3,0,2:T(8,128)(2,1)S(1)} %get-tuple-element.45) | copy-start | bytes 12292
  110.6 7.5 copy-start.6
  110.6 7.6 copy-start.7
  110.6 19.9 %all-to-all-start = ((bf16[8,2,32768]{2,1,0:T(2,128)(2,1)}), bf16[8,2,32768]{2,1,0:T(2,128)(2,1)S(1)}, u32[]{:S(2)}, u32[]{:S(2)}) async-start(bf16[8,2,32768]{2,1,0:T(2,128)(2,1)} %reshape.284), calls=%async_computation | async-start | bytes 2097152 | tf_op jit(solution)/shard_map/all_to_all | solution.py:83
  116.1 18.9 %copy-start.12 = (s32[256]{0:T(256)}, s32[256]{0:T(256)S(1)}, u32[]{:S(2)}) copy-start(s32[256]{0:T(256)S(1)} %and_select_fusion) | copy-start | bytes 3076
  141.8 5.4 copy-start.5
  165.9 19.4 %all-to-all-start.1 = ((bf16[8,2,32768]{2,1,0:T(2,128)(2,1)}), bf16[8,2,32768]{2,1,0:T(2,128)(2,1)S(1)}, u32[]{:S(2)}, u32[]{:S(2)}) async-start(bf16[8,2,32768]{2,1,0:T(2,128)(2,1)} %reshape.286), calls=%async_computation.1 | async-start | bytes 2097152 | tf_op jit(solution)/shard_map/all_to_all | solution.py:100
  170.9 184.8 %all-reduce.6.cloned.1.call-start = ((), (), s32[]{:S(2)}) async-start(), calls=%async_computation.10 | async-start | bytes 2097152
  202.2 1.0 copy-start.3
  203.2 1.6 copy-start
  206.7 1.7 copy-start.14
  206.8 148.9 %copy-start.1 = (f32[1,2,32,256]{3,2,1,0:T(8,128)S(1)}, f32[1,2,32,256]{3,2,1,0:T(8,128)}, u32[]{:S(2)}) copy-start(f32[1,2,32,256]{3,2,1,0:T(8,128)} %param.6) | copy-start | bytes 196612
  208.3 375.2 %all-gather.7.cloned.1.call-start = ((), (), s32[]{:S(2)}) async-start(), calls=%async_computation.7 | async-start | bytes 1081344 | tf_op jit(solution)/shard_map/all_gather | solution.py:77
  510.2 338.9 %all-reduce.8.cloned.1.call-start = ((), (), s32[]{:S(2)}) async-start(), calls=%async_computation.11 | async-start | bytes 2097152
  697.9 1.0 copy-start.4
  700.4 226.5 %copy-start.9 = (bf16[1,32,2,32]{1,3,0,2:T(8,128)(2,1)S(1)}, bf16[1,32,2,32]{1,3,0,2:T(8,128)(2,1)}, u32[]{:S(2)}) copy-start(bf16[1,32,2,32]{1,3,0,2:T(8,128)(2,1)} %copy-done.8) | copy-start | bytes 12292
  700.4 226.5 %copy-start.11 = (bf16[1,32,2,32]{1,3,0,2:T(8,128)(2,1)S(1)}, bf16[1,32,2,32]{1,3,0,2:T(8,128)(2,1)}, u32[]{:S(2)}) copy-start(bf16[1,32,2,32]{1,3,0,2:T(8,128)(2,1)} %copy-done.10) | copy-start | bytes 12292
  702.0 298.7 %all-gather.9.cloned.1.call-start = ((), (), s32[]{:S(2)}) async-start(), calls=%async_computation.8 | async-start | bytes 1081344 | tf_op jit(solution)/shard_map/all_gather | solution.py:77
  943.6 77.2 %all-to-all-start.5 = ((bf16[8,2,32768]{2,1,0:T(2,128)(2,1)}), bf16[8,2,32768]{2,1,0:T(2,128)(2,1)S(1)}, u32[]{:S(2)}, u32[]{:S(2)}) async-start(bf16[8,2,32768]{2,1,0:T(2,128)(2,1)} %reshape.294), calls=%async_computation.5 | async-start | bytes 2097152 | tf_op jit(solution)/shard_map/all_to_all | solution.py:83
  1020.7 25.9 %all-to-all-start.4 = ((bf16[8,2,32768]{2,1,0:T(2,128)(2,1)}), bf16[8,2,32768]{2,1,0:T(2,128)(2,1)}, u32[]{:S(2)}, u32[]{:S(2)}) async-start(bf16[8,2,32768]{2,1,0:T(2,128)(2,1)} %reshape.292), calls=%async_computation.4 | async-start | bytes 2097152 | tf_op jit(solution)/shard_map/all_to_all | solution.py:83
  1065.6 1.8 copy-start.2
  1065.6 1.8 copy-start.13
Sparse Core Ops, SparseCore 0:
  11.1 79.3 all-gather.4
  93.1 73.7 all-gather.10
  208.5 147.1 all-reduce.5
  510.3 73.2 all-gather.6
  702.1 146.9 all-reduce.7
  927.0 73.6 all-gather.8
where the time goes:
time: 1230 us; the launch traced here: 1220 us
  waiting for transfers between devices  514 us (42%)
  blocking collectives  398 us (32%)
  local copies, waits for them, and re-layouts  199 us (16%)
  other arithmetic  41.5 us (3%)
  matrix products  24.6 us (2%)
  starting transfers between devices  21.6 us (2%)
  between operations  18.5 us (2%)
    unnamed x8, waiting for transfers between devices  294 us
    all_gather x4, waiting for transfers between devices, gathered_front(): return front(lax.all_gather(shard, 'coil', axis=0, tiled=True))  198 us
    psum x2, blocking collectives, inner_norm(): return lax.psum(jnp.sum(values * values), ('coil', 'slab'))  146 us
    psum x1, blocking collectives, shards(): logit_grad = lax.psum(partial_grad, 'coil')  140 us
    unnamed x44, local copies, waits for them, and re-layouts  82.7 us
    psum x1, blocking collectives, shards(): alpha = norm_now / lax.psum(jnp.sum(direction * image), ('coil', 'slab'))  72.6 us
    all_to_all x8, local copies, waits for them, and re-layouts, to_kspace(): lax.all_to_all(mixed, 'slab', split_axis=3, concat_axis=2, tiled=True)  48.2 us
    convert_element_type x4, local copies, waits for them, and re-layouts, to_kspace(): mixed = jnp.einsum('nixk,inom->moxk', rows, z_fwd, preferred_element_type...  26.2 us
  transfers between devices with their start and end apart: 10, of which 7 were waited for; matrix products, arithmetic and copies ran while one was open for 11% of the time, Pallas kernels for 0%

commit v1 on v0

--- a/solution.py
+++ b/solution.py
@@ -83,52 +83,61 @@
         swapped = lax.all_to_all(mixed, "slab", split_axis=3, concat_axis=2, tiled=True)
         return jnp.einsum("zink,inoq->zokq", swapped, x_fwd, preferred_element_type=jnp.float32)
 
-    residual = cotangent
+    direction = cotangent
+    both = ("coil", "slab")
+    saved_k = to_kspace(gathered_front(saved_solution.astype(jnp.bfloat16)))
+    first_k = to_kspace(gathered_front(direction.astype(jnp.bfloat16)))
+    first_w = weight[:, None] * first_k
+    norm_now, first_energy = lax.psum(
+        (jnp.sum(direction * direction), jnp.sum(first_w * first_w)), both
+    )
+    apply_spectrum = (squared * first_k).astype(jnp.bfloat16)
+    to_mixed = jnp.einsum(
+        "zikq,iqon->zonk", apply_spectrum, x_inv, preferred_element_type=jnp.float32
+    ).astype(jnp.bfloat16)
+    to_swapped = lax.all_to_all(to_mixed, "slab", split_axis=2, concat_axis=3, tiled=True)
+    apply_image_rows = jnp.einsum(
+        "mixk,imon->noxk", to_swapped, z_inv, preferred_element_type=jnp.float32
+    ).astype(jnp.bfloat16)
+    image = jnp.einsum(
+        "zixk,ikon->zoxn", apply_image_rows, y_inv, preferred_element_type=jnp.float32
+    )
+    summed = lax.psum_scatter(
+        conjugate_product(maps.astype(jnp.float32), image).astype(jnp.bfloat16),
+        "coil",
+        scatter_dimension=0,
+        tiled=True,
+    ).astype(jnp.float32)
+    image = summed + DAMPING * direction
+    alpha = norm_now / (first_energy + DAMPING * norm_now)
+    residual = direction - alpha * image
+    second_k = to_kspace(gathered_front(residual.astype(jnp.bfloat16)))
+    second_w = weight[:, None] * second_k
+    gain = gate * (1.0 - gate)
+    target = data - 2.0 * weight[:, None] * saved_k
 
-    def inner_norm(values):
-        return lax.psum(jnp.sum(values * values), ("coil", "slab"))
+    def line_terms(spectrum):
+        return gain * jnp.sum(sampled * jnp.sum(spectrum * target, axis=1), axis=2)
 
-    direction = residual
-    solution = jnp.zeros(residual.shape, jnp.float32)
-    norm_now = inner_norm(residual)
-    for step in range(ITERS):
-        apply_rows = gathered_front(direction.astype(jnp.bfloat16))
-        apply_spectrum = (squared * to_kspace(apply_rows)).astype(jnp.bfloat16)
-        to_mixed = jnp.einsum(
-            "zikq,iqon->zonk", apply_spectrum, x_inv, preferred_element_type=jnp.float32
-        ).astype(jnp.bfloat16)
-        to_swapped = lax.all_to_all(to_mixed, "slab", split_axis=2, concat_axis=3, tiled=True)
-        apply_image_rows = jnp.einsum(
-            "mixk,imon->noxk", to_swapped, z_inv, preferred_element_type=jnp.float32
-        ).astype(jnp.bfloat16)
-        image = jnp.einsum(
-            "zixk,ikon->zoxn", apply_image_rows, y_inv, preferred_element_type=jnp.float32
-        )
-        summed = lax.psum_scatter(
-            conjugate_product(maps.astype(jnp.float32), image).astype(jnp.bfloat16),
-            "coil",
-            scatter_dimension=0,
-            tiled=True,
-        ).astype(jnp.float32)
-        image = summed + DAMPING * direction
-        alpha = norm_now / lax.psum(jnp.sum(direction * image), ("coil", "slab"))
-        solution = solution + alpha * direction
-        if step + 1 < ITERS:
-            residual = residual - alpha * image
-            norm_next = inner_norm(residual)
-            direction = residual + norm_next / norm_now * direction
-            norm_now = norm_next
-    image_grad = DAMPING * solution
-    solution_rows = gathered_front(solution.astype(jnp.bfloat16))
-    saved_rows = gathered_front(saved_solution.astype(jnp.bfloat16))
-    solution_k = to_kspace(solution_rows)
-    saved_k = to_kspace(saved_rows)
-    kspace_grad = (weight[:, None] * solution_k).astype(jnp.bfloat16)[None]
-    value = solution_k[:, 0] * (data[:, 0] - 2.0 * weight * saved_k[:, 0]) + solution_k[:, 1] * (
-        data[:, 1] - 2.0 * weight * saved_k[:, 1]
+    norm_next, crossing, second_energy, mixed_energy = lax.psum(
+        (
+            jnp.sum(residual * residual),
+            jnp.sum(residual * direction),
+            jnp.sum(second_w * second_w),
+            jnp.sum(second_w * first_w),
+        ),
+        both,
     )
-    partial_grad = gate * (1.0 - gate) * jnp.sum(sampled * value, axis=2)
-    logit_grad = lax.psum(partial_grad, "coil")
+    lines = lax.psum(jnp.stack([line_terms(first_k), line_terms(second_k)]), "coil")
+    beta = norm_next / norm_now
+    curvature = (second_energy + beta * (2.0 * mixed_energy + beta * first_energy)) + DAMPING * (
+        norm_next + beta * (2.0 * crossing + beta * norm_now)
+    )
+    later = norm_next / curvature
+    early = alpha + later * beta
+    image_grad = DAMPING * (early * direction + later * residual)
+    kspace_grad = (early * first_w + later * second_w).astype(jnp.bfloat16)[None]
+    logit_grad = early * lines[0] + later * lines[1]
     return (image_grad, kspace_grad, logit_grad)
 
 

time: 1230 us -> 763 us (0.62)
  waiting for transfers between devices: 514 us -> 219 us
  blocking collectives: 398 us -> 288 us
  local copies, waits for them, and re-layouts: 199 us -> 143 us
    unnamed x8 -> x5, waiting for transfers between devices: 294 us -> 71 us
    all_gather x4 -> x3, waiting for transfers between devices: 198 us -> 125 us  [gathered_front(): return front(lax.all_gather(shard, 'coil', axis=0, tiled=True))]
    psum x4 -> x3, blocking collectives: 359 us -> 288 us  [the longest x1 140 us: shards(): lax.psum(jnp.stack([line_terms(first_k), line_terms(second_k)]), 'coil')]
    all_to_all x2 -> x0, blocking collectives: 38.8 us -> none  [the longest x1 19.5 us: shards(): lax.all_to_all(to_mixed, 'slab', split_axis=2, concat_axis=3, tiled=True)]
    unnamed x44 -> x30, local copies, waits for them, and re-layouts: 82.7 us -> 61.8 us
    all_to_all x8 -> x6, local copies, waits for them, and re-layouts: 48.2 us -> 38.1 us  [to_kspace(): lax.all_to_all(mixed, 'slab', split_axis=3, concat_axis=2, tiled=True)]
    convert_element_type x4 -> x3, local copies, waits for them, and re-layouts: 26.2 us -> 21 us  [to_kspace(): mixed = jnp.einsum('nixk,inom->moxk', rows, z_fwd, preferred_element_type...]
  transfers between devices with their start and end apart: 10 -> 8, of which waited for: 7 -> 5; matrix products, arithmetic and copies ran while one was open for 11% -> 18% of each run, Pallas kernels for 0% -> 0%
where the time goes in v1:
time: 763 us; the launch traced here: 753 us
  blocking collectives  288 us (38%)
  waiting for transfers between devices  219 us (29%)
  local copies, waits for them, and re-layouts  143 us (19%)
  other arithmetic  33.3 us (4%)
  matrix products  27.2 us (4%)
  between operations  22.1 us (3%)
  starting transfers between devices  21 us (3%)
    psum x1, blocking collectives, shards(): lax.psum(jnp.stack([line_terms(first_k), line_terms(second_k)]), 'coil')  140 us
    all_gather x3, waiting for transfers between devices, gathered_front(): return front(lax.all_gather(shard, 'coil', axis=0, tiled=True))  125 us
    psum x1, blocking collectives, shards(): lax.psum((jnp.sum(residual * residual), jnp.sum(residual * direction), jn...  74.5 us
    psum x1, blocking collectives, shards(): lax.psum((jnp.sum(direction * direction), jnp.sum(first_w * first_w)), both)  73.8 us
    unnamed x5, waiting for transfers between devices  71 us
    unnamed x30, local copies, waits for them, and re-layouts  61.8 us
    all_to_all x6, local copies, waits for them, and re-layouts, to_kspace(): lax.all_to_all(mixed, 'slab', split_axis=3, concat_axis=2, tiled=True)  38.1 us
    convert_element_type x3, local copies, waits for them, and re-layouts, to_kspace(): mixed = jnp.einsum('nixk,inom->moxk', rows, z_fwd, preferred_element_type...  21 us
  transfers between devices with their start and end apart: 8, of which 5 were waited for; matrix products, arithmetic and copies ran while one was open for 18% of the time, Pallas kernels for 0%

profile of v1, /device:TPU:2, one launch (start us, length us, event | category | flops | bytes accessed | tf_op | source)
XLA Modules:
  0.0 753.4 jit_solution(7913596652548034315)
XLA Ops:
  7.2 2.1 fusion.89
  9.4 1.4 convert_element_type.210
  10.9 1.0 negate_convert_fusion
  11.9 1.1 multiply_convert_fusion
  13.0 1.0 multiply_convert_fusion.2
  14.3 1.8 bitcast_convert_fusion.8
  16.2 74.3 %all-gather.4.cloned.1.call-done = bf16[32,2,32,256]{3,2,1,0:T(8,128)(2,1)} async-done(((bf16[1,2,32,256]{3,2,1,0:T(8,128)(2,1)}), bf16[32,2,32,256]{3,2,1,0:T(8,128)(2,1)}) %all-gather.4.cloned.1.call-update) | async-done | bytes 1048592 | tf_op jit(solution)/shard_map/all_gather | solution.py:77
  90.6 1.8 copy_convert_fusion.2
  92.4 1.5 subtract_convert_fusion.3
  93.9 3.2 fusion.4
  97.1 7.2 copy.81
  104.3 7.8 %reshape.272 = bf16[8,2,32768]{2,1,0:T(2,128)(2,1)} reshape(bf16[256,2,32,32]{3,2,1,0:T(8,128)(2,1)} %bitcast.296) | data formatting | bytes 2097152
  112.2 5.2 all-to-all-start
  117.3 1.1 pad_maximum_fusion.2
  118.4 1.7 fusion.32
  120.1 11.7 %all-to-all-done = bf16[8,2,32768]{2,1,0:T(2,128)(2,1)} async-done(((bf16[8,2,32768]{2,1,0:T(2,128)(2,1)}), bf16[8,2,32768]{2,1,0:T(2,128)(2,1)}, u32[]{:S(2)}, u32[]{:S(2)}) %all-to-all-start) | async-done | bytes 1048608 | tf_op jit(solution)/shard_map/all_to_all | solution.py:83
  131.8 7.0 reshape.273
  138.9 6.8 copy.82
  145.6 6.2 reshape.243
  151.8 4.4 fusion.2
  156.2 1.7 fusion.9
  157.9 7.2 copy.85
  165.1 7.8 %reshape.274 = bf16[8,2,32768]{2,1,0:T(2,128)(2,1)} reshape(bf16[256,2,32,32]{3,2,1,0:T(8,128)(2,1)} %bitcast.297) | data formatting | bytes 2097152
  172.9 5.5 all-to-all-start.1
  178.7 3.2 copy_convert_fusion
  181.9 11.2 %all-to-all-done.1 = bf16[8,2,32768]{2,1,0:T(2,128)(2,1)} async-done(((bf16[8,2,32768]{2,1,0:T(2,128)(2,1)}), bf16[8,2,32768]{2,1,0:T(2,128)(2,1)}, u32[]{:S(2)}, u32[]{:S(2)}) %all-to-all-start.1) | async-done | bytes 1048608 | tf_op jit(solution)/shard_map/all_to_all | solution.py:98
  193.1 7.0 reshape.275
  200.1 6.9 copy.160
  207.0 6.2 all_to_all.59
  213.1 2.2 fusion.5
  215.3 0.7 convolution_bitcast_fusion
  216.0 0.9 copy-done.1
  216.9 1.9 subtract_convert_fusion
  219.0 1.6 copy.92
  220.6 0.6 dynamic-slice
  221.2 73.8 %all-reduce.2 = (f32[]{:T(128)}, f32[]{:T(128)}) all-reduce(f32[]{:T(128)} %get-tuple-element.49, f32[]{:T(128)} %get-tuple-element.40), channel_id=1, replica_groups=mesh['coil'=32,'slab'=8] {'coil','slab'}, use_global_device_ids=true, to_apply=%region_1.2 | all-reduce | flops 2 | bytes 16 | tf_op jit(solution)/shard_map/psum | solution.py:91
  296.9 71.0 %all-reduce.5.cloned.1.call-done = bf16[32,2,32,256]{3,2,0,1:T(8,128)(2,1)} async-done(((bf16[32,2,32,256]{3,2,0,1:T(8,128)(2,1)}), bf16[32,2,32,256]{3,2,0,1:T(8,128)(2,1)}) %all-reduce.5.cloned.1.call-update) | async-done | bytes 1048592
  367.9 2.7 fusion.61
  370.6 3.3 fusion.7
  373.9 7.2 copy.103
  381.1 7.8 %reshape.278 = bf16[8,2,32768]{2,1,0:T(2,128)(2,1)} reshape(bf16[256,2,32,32]{3,2,1,0:T(8,128)(2,1)} %bitcast.298) | data formatting | bytes 2097152
  388.9 5.1 all-to-all-start.3
  394.0 50.5 %all-gather.6.cloned.1.call-done = bf16[32,2,32,256]{3,2,1,0:T(8,128)(2,1)} async-done(((bf16[1,2,32,256]{3,2,1,0:T(8,128)(2,1)}), bf16[32,2,32,256]{3,2,1,0:T(8,128)(2,1)}) %all-gather.6.cloned.1.call-update) | async-done | bytes 1048592 | tf_op jit(solution)/shard_map/all_gather | solution.py:77
  444.5 1.8 copy_convert_fusion.1
  446.4 1.5 subtract_convert_fusion.1
  447.9 2.3 fusion.6
  450.2 6.5 copy.97
  456.7 7.8 %reshape.276 = bf16[8,2,32768]{2,1,0:T(2,128)(2,1)} reshape(bf16[256,2,32,32]{3,2,1,0:T(8,128)(2,1)} %bitcast.299) | data formatting | bytes 2097152
  464.5 4.8 all-to-all-start.2
  469.3 7.0 reshape.279
  476.3 6.7 copy.104
  483.0 5.4 reshape.264
  488.4 3.4 fusion
  491.8 7.0 reshape.277
  498.8 6.7 copy.98
  505.5 6.3 reshape.258
  511.9 6.2 multiply_reduce_fusion
  518.0 74.5 %all-reduce.1 = (f32[]{:T(128)}, f32[]{:T(128)}, f32[]{:T(128)}, f32[]{:T(128)}) all-reduce(f32[]{:T(128)} %get-tuple-element.20, f32[]{:T(128)} %get-tuple-element.16, f32[]{:T(128)} %get-tuple-element.15, f32[]{:T(128)} %get-tuple-element.19), channel_id=1, replica_groups=mesh['coil'=32,'slab'=8] {'coil','slab'}, use_global_device_ids=true, to_apply=%region_6.7 | all-reduce | flops 4 | bytes 32 | tf_op jit(solution)/shard_map/psum | solution.py:122
  595.0 2.1 fusion.12
  597.2 140.0 %psum.55 = f32[2,32,32]{2,1,0:T(8,128)S(1)} all-reduce(f32[2,32,32]{2,1,0:T(8,128)S(1)} %pad_maximum_fusion.7), channel_id=1, replica_groups=mesh['coil'=32,'slab'=8] {'coil'}, use_global_device_ids=true, to_apply=%region_17.18 | all-reduce | flops 2048 | bytes 16384 | tf_op jit(solution)/shard_map/psum | solution.py:131
  740.4 0.6 fusion.76
  741.0 2.3 fusion.14
  743.3 1.1 copy.106
  744.4 2.0 fusion.64
  (41 shorter events, 1.0 us)
Async XLA Ops:
  7.2 83.4 %all-gather.4.cloned.1.call-start = ((), (), s32[]{:S(2)}) async-start(), calls=%async_computation.4 | async-start | bytes 1081344 | tf_op jit(solution)/shard_map/all_gather | solution.py:77
  9.4 169.3 %all-gather.8.cloned.1.call-start = ((), (), s32[]{:S(2)}) async-start(), calls=%async_computation.6 | async-start | bytes 1081344 | tf_op jit(solution)/shard_map/all_gather | solution.py:77
  16.2 77.7 %copy-start.3 = (bf16[1,256,2,256]{3,1,0,2:T(8,128)(2,1)}, bf16[1,256,2,256]{3,1,0,2:T(8,128)(2,1)S(1)}, u32[]{:S(2)}) copy-start(bf16[1,256,2,256]{3,1,0,2:T(8,128)(2,1)S(1)} %get-tuple-element.47) | copy-start | bytes 786436
  112.1 6.3 copy-start.8
  112.2 6.3 copy-start.7
  112.2 19.7 %all-to-all-start = ((bf16[8,2,32768]{2,1,0:T(2,128)(2,1)}), bf16[8,2,32768]{2,1,0:T(2,128)(2,1)}, u32[]{:S(2)}, u32[]{:S(2)}) async-start(bf16[8,2,32768]{2,1,0:T(2,128)(2,1)} %reshape.272), calls=%async_computation | async-start | bytes 2097152 | tf_op jit(solution)/shard_map/all_to_all | solution.py:83
  151.8 4.4 copy-start.6
  172.9 20.2 %all-to-all-start.1 = ((bf16[8,2,32768]{2,1,0:T(2,128)(2,1)}), bf16[8,2,32768]{2,1,0:T(2,128)(2,1)}, u32[]{:S(2)}, u32[]{:S(2)}) async-start(bf16[8,2,32768]{2,1,0:T(2,128)(2,1)} %reshape.274), calls=%async_computation.1 | async-start | bytes 2097152 | tf_op jit(solution)/shard_map/all_to_all | solution.py:98
  178.5 189.4 %all-reduce.5.cloned.1.call-start = ((), (), s32[]{:S(2)}) async-start(), calls=%async_computation.7 | async-start | bytes 2097152
  213.1 2.2 copy-start.5
  215.3 1.6 copy-start.1
  218.9 1.7 copy-start.9
  218.9 148.9 %copy-start.4 = (f32[1,2,32,256]{3,2,1,0:T(8,128)S(1)}, f32[1,2,32,256]{3,2,1,0:T(8,128)}, u32[]{:S(2)}) copy-start(f32[1,2,32,256]{3,2,1,0:T(8,128)} %param.6) | copy-start | bytes 196612
  220.6 224.0 %all-gather.6.cloned.1.call-start = ((), (), s32[]{:S(2)}) async-start(), calls=%async_computation.5 | async-start | bytes 1081344 | tf_op jit(solution)/shard_map/all_gather | solution.py:77
  388.9 75.6 %all-to-all-start.3 = ((bf16[8,2,32768]{2,1,0:T(2,128)(2,1)}), bf16[8,2,32768]{2,1,0:T(2,128)(2,1)}, u32[]{:S(2)}, u32[]{:S(2)}) async-start(bf16[8,2,32768]{2,1,0:T(2,128)(2,1)} %reshape.278), calls=%async_computation.3 | async-start | bytes 2097152 | tf_op jit(solution)/shard_map/all_to_all | solution.py:83
  464.5 27.3 %all-to-all-start.2 = ((bf16[8,2,32768]{2,1,0:T(2,128)(2,1)}), bf16[8,2,32768]{2,1,0:T(2,128)(2,1)}, u32[]{:S(2)}, u32[]{:S(2)}) async-start(bf16[8,2,32768]{2,1,0:T(2,128)(2,1)} %reshape.276), calls=%async_computation.2 | async-start | bytes 2097152 | tf_op jit(solution)/shard_map/all_to_all | solution.py:83
  483.0 5.4 copy-start.2
  505.5 6.3 copy-start
Sparse Core Ops, SparseCore 0:
  11.1 79.3 all-gather.3
  93.1 73.8 all-gather.7
  220.7 147.1 all-reduce.4
  370.9 73.5 all-gather.5

commit v2 on v1

v2 whole, which is shorter than its diff:
```python
import jax
import jax.numpy as jnp
import numpy as np
from jax import lax
from jax.experimental import pallas as pl
from jax.experimental.pallas import tpu as pltpu
from jax.sharding import PartitionSpec as P

N = 256
NZ = 32
DAMPING = 0.2
DEPTH = 8
BREADTH = 4
NEAREST = (1, 7, 2, 6, 3, 5, 4)
MESH = pl.DeviceIdType.MESH
BF16 = jnp.bfloat16
F32 = jnp.float32


def tables():
    def cosine_sine(length):
        index = np.arange(length)
        phase = (index[:, None] * index[None, :] % length).astype(np.float32) * np.float32(
            2.0 * np.pi / length
        )
        factor = np.float32(1.0 / np.sqrt(length))
        return np.cos(phase) * factor, np.sin(phase) * factor

    plane = np.stack(cosine_sine(N))
    eye = np.eye(8, dtype=np.float32)
    depth = np.stack([np.kron(part, eye) for part in cosine_sine(NZ)])
    return jnp.asarray(plane, BF16), jnp.asarray(depth, BF16)


def dot(left, right, dims=((1,), (0,))):
    return lax.dot_general(left, right, (dims, ((), ())), preferred_element_type=F32)


def call(body, out_shape, scratch=(), collective=None, name=None):
    params = dict(vmem_limit_bytes=60 * 1024 * 1024)
    if collective is not None:
        params.update(collective_id=collective, has_side_effects=True)
    many = isinstance(out_shape, (tuple, list))

    def run(*args):
        return pl.pallas_call(
            body,
            out_shape=out_shape,
            in_specs=[pl.BlockSpec(memory_space=pltpu.VMEM)] * len(args),
            out_specs=[pl.BlockSpec(memory_space=pltpu.VMEM)] * len(out_shape)
            if many
            else pl.BlockSpec(memory_space=pltpu.VMEM),
            scratch_shapes=list(scratch),
            compiler_params=pltpu.CompilerParams(**params),
            name=name,
        )(*args)

    return run


class Place:
    def __init__(self):
        self.coil = lax.axis_index("coil")
        self.slab = lax.axis_index("slab")
        self.z, self.y = self.coil // BREADTH, self.coil % BREADTH
        self.x, self.core = self.slab // 2, self.slab % 2

    def along_z(self, step):
        return ((self.z + step + DEPTH) % DEPTH) * BREADTH + self.y

    def along_y(self, step):
        return self.z * BREADTH + self.row(step)

    def row(self, step):
        return (self.y + step + BREADTH) % BREADTH

    def along_x(self, step, core):
        return ((self.x + step + 4) % 4) * 2 + core


def greet(place, planes, slabs, rows=False):
    barrier = pltpu.get_barrier_semaphore()
    targets = []
    if planes:
        targets += [(place.along_z(step), place.slab) for step in range(1, DEPTH)]
        targets += [(place.along_y(step), place.slab) for step in ((1, 2, 3) if rows else (1, 3))]
    if slabs:
        targets += [(place.coil, place.along_x(step, core)) for step in (1, 3) for core in (0, 1)]
        targets += [(place.coil, place.along_x(0, 1 - place.core))]
        if slabs > 1:
            targets += [(place.coil, place.along_x(2, core)) for core in (0, 1)]
    for target in targets:
        pl.semaphore_signal(barrier, inc=1, device_id=target, device_id_type=MESH)
    pl.semaphore_wait(barrier, len(targets))


def sender(sends, receives):
    started = []

    def start(source, target, number, arrival, device):
        copy = pltpu.make_async_remote_copy(
            src_ref=source,
            dst_ref=target,
            send_sem=sends.at[number],
            recv_sem=receives.at[arrival],
            device_id=device,
            device_id_type=MESH,
        )
        copy.start()
        started.append(copy)

    def arrived(target, arrival, device):
        pltpu.make_async_remote_copy(
            src_ref=target,
            dst_ref=target,
            send_sem=sends.at[0],
            recv_sem=receives.at[arrival],
            device_id=device,
            device_id_type=MESH,
        ).wait_recv()

    def drain():
        for copy in started:
            copy.wait_send()

    return start, arrived, drain


class Exchange:
    COPIES = 13

    def __init__(self, place, source, target, relay, sends, receives):
        self.p, self.source, self.target, self.relay = place, source, target, relay
        self.start, self.arrived, self.drain = sender(sends, receives)

    @staticmethod
    def scratch():
        return [
            pltpu.VMEM((2, 2, 2, 2, 32, N), BF16),
            pltpu.SemaphoreType.DMA((Exchange.COPIES,)),
            pltpu.SemaphoreType.DMA((Exchange.COPIES,)),
        ]

    def begin(self):
        p = self.p
        for way, step in ((0, 1), (1, -1)):
            for core in (0, 1):
                self.start(
                    self.source.at[p.along_x(2, core), pl.ds(2 * way, 2)],
                    self.relay.at[way, core],
                    way * 2 + core,
                    way * 2 + core,
                    (p.coil, p.along_x(step, p.core)),
                )
        for way, step in ((0, 1), (1, -1)):
            for core in (0, 1):
                self.start(
                    self.source.at[p.along_x(step, core)],
                    self.target.at[p.slab],
                    4 + way * 2 + core,
                    4 + way * 2 + p.core,
                    (p.coil, p.along_x(step, core)),
                )
        partner = p.along_x(0, 1 - p.core)
        self.start(self.source.at[partner], self.target.at[p.slab], 12, 12, (p.coil, partner))
        self.target[p.slab] = self.source[p.slab]

    def forward(self):
        p = self.p
        for way, step in ((0, 1), (1, -1)):
            for core in (0, 1):
                self.arrived(
                    self.relay.at[way, core], way * 2 + core, (p.coil, p.along_x(-step, p.core))
                )
                self.start(
                    self.relay.at[way, core],
                    self.target.at[p.along_x(-step, p.core), pl.ds(2 * way, 2)],
                    8 + way * 2 + core,
                    8 + way * 2 + p.core,
                    (p.coil, p.along_x(step, core)),
                )

    def finish(self):
        p = self.p
        partner = p.along_x(0, 1 - p.core)
        self.arrived(self.target.at[partner], 12, (p.coil, partner))
        for way, step in ((0, 1), (1, -1)):
            for core in (0, 1):
                near = p.along_x(-step, core)
                self.arrived(self.target.at[near], 4 + way * 2 + core, (p.coil, near))
        for way, step in ((0, 1), (1, -1)):
            for core in (0, 1):
                far = p.along_x(2, core)
                self.arrived(
                    self.target.at[far, pl.ds(2 * way, 2)], 8 + way * 2 + core, (p.coil, far)
                )
        self.drain()


class Gather:
    COPIES = 39

    def __init__(self, place, source, target, sends, receives):
        self.p, self.source, self.target = place, source, target
        self.start, self.arrived, self.drain = sender(sends, receives)

    @staticmethod
    def scratch():
        return [
            pltpu.SemaphoreType.DMA((Gather.COPIES,)),
            pltpu.SemaphoreType.DMA((Gather.COPIES,)),
        ]

    def slice_of(self, order, row_step):
        p = self.p
        back = 0 if order == 0 else NEAREST[order - 1]
        return ((p.z - back + DEPTH) % DEPTH) * BREADTH + p.row(row_step)

    def pass_on(self, order, source):
        p = self.p
        slot = self.slice_of(order, 0)
        for way, step in ((0, 1), (1, -1)):
            number = 7 + order * 2 + way
            self.start(source, self.target.at[slot], number, number, (p.along_y(step), p.slab))

    def begin(self):
        p = self.p
        for order, step in enumerate(NEAREST):
            self.start(
                self.source, self.target.at[p.coil], order, order, (p.along_z(step), p.slab)
            )
        self.pass_on(0, self.source)
        self.target[p.coil] = self.source[...]

    def spread(self):
        p = self.p
        for order, step in enumerate(NEAREST):
            slot = self.slice_of(order + 1, 0)
            self.arrived(self.target.at[slot], order, (p.along_z(-step), p.slab))
            self.pass_on(order + 1, self.target.at[slot])

    def forward(self):
        p = self.p
        for order in range(DEPTH):
            for way, step in ((0, 1), (1, -1)):
                slot = self.slice_of(order, -step)
                self.arrived(
                    self.target.at[slot], 7 + order * 2 + way, (p.along_y(-step), p.slab)
                )
                number = 23 + order * 2 + way
                half = self.target.at[slot, pl.ds(way, 1)]
                self.start(half, half, number, number, (p.along_y(step), p.slab))

    def finish(self):
        p = self.p
        for order in range(DEPTH):
            for way, step in ((0, 1), (1, -1)):
                slot = self.slice_of(order, 2)
                self.arrived(
                    self.target.at[slot, pl.ds(way, 1)],
                    23 + order * 2 + way,
                    (p.along_y(-step), p.slab),
                )
        self.drain()


class Scatter:
    COPIES = 13

    def __init__(self, place, terms, far, near, mixed, rows, column, sends, receives):
        self.p, self.terms = place, terms
        self.far, self.near, self.mixed, self.rows, self.column = far, near, mixed, rows, column
        self.start, self.arrived, self.drain = sender(sends, receives)

    @staticmethod
    def scratch():
        return [
            pltpu.VMEM((2, DEPTH, 32, N), BF16),
            pltpu.VMEM((2, 2, DEPTH, 32, N), BF16),
            pltpu.VMEM((2, DEPTH, 32, N), BF16),
            pltpu.VMEM((DEPTH, 2, 32, N), BF16),
            pltpu.VMEM((DEPTH - 1, 2, 32, N), BF16),
            pltpu.SemaphoreType.DMA((Scatter.COPIES,)),
            pltpu.SemaphoreType.DMA((Scatter.COPIES,)),
        ]

    def begin(self):
        p = self.p
        for way, step in ((0, 1), (1, -1)):
            beside = (p.along_y(step), p.slab)
            self.start(self.terms.at[:, p.row(2), way], self.far.at[way], way, way, beside)
        for way, step in ((0, 1), (1, -1)):
            beside = (p.along_y(step), p.slab)
            self.start(
                self.terms.at[:, p.row(step), 1 - way],
                self.near.at[way, 1 - way],
                2 + way,
                2 + way,
                beside,
            )

    def forward(self):
        p = self.p
        for way, step in ((0, 1), (1, -1)):
            beside = (p.along_y(step), p.slab)
            self.arrived(self.far.at[way], way, (p.along_y(-step), p.slab))
            self.mixed[way] = (
                self.far[way].astype(F32) + self.terms[:, p.row(step), way].astype(F32)
            ).astype(BF16)
            self.start(self.mixed.at[way], self.near.at[way, way], 4 + way, 4 + way, beside)

    def columns(self):
        p = self.p
        for way, step in ((0, 1), (1, -1)):
            beside = (p.along_y(-step), p.slab)
            self.arrived(self.near.at[way, 1 - way], 2 + way, beside)
            self.arrived(self.near.at[way, way], 4 + way, beside)
        for part in (0, 1):
            self.rows[:, part] = (
                self.terms[:, p.row(0), part].astype(F32)
                + self.near[0, part].astype(F32)
                + self.near[1, part].astype(F32)
            ).astype(BF16)
        for order, step in enumerate(NEAREST):
            self.start(
                self.rows.at[(p.z + step) % DEPTH],
                self.column.at[order],
                6 + order,
                6 + order,
                (p.along_z(step), p.slab),
            )

    def total(self):
        p = self.p
        value = self.rows[p.z].astype(F32)
        for order, step in enumerate(NEAREST):
            self.arrived(self.column.at[order], 6 + order, (p.along_z(-step), p.slab))
            value = value + self.column[order].astype(F32)
        return value


class Total:
    COPIES = 17

    def __init__(self, place, held, shared, sends, receives):
        self.p, self.held, self.shared = place, held, shared
        self.start, self.arrived, self.drain = sender(sends, receives)

    @staticmethod
    def scratch(height, shared):
        return [
            pltpu.VMEM((12, height, 128), F32),
            pltpu.VMEM((8, shared, 128), F32),
            pltpu.SemaphoreType.DMA((Total.COPIES,)),
            pltpu.SemaphoreType.DMA((Total.COPIES,)),
        ]

    def along_z(self, value):
        p = self.p
        self.held[p.z] = value
        for order, step in enumerate(NEAREST):
            self.start(
                self.held.at[p.z], self.held.at[p.z], order, order, (p.along_z(step), p.slab)
            )

    def sum_z(self):
        p = self.p
        for order, step in enumerate(NEAREST):
            self.arrived(
                self.held.at[(p.z - step + DEPTH) % DEPTH], order, (p.along_z(-step), p.slab)
            )
        value = self.held[0]
        for place in range(1, DEPTH):
            value = value + self.held[place]
        return value

    def along_y(self, value):
        p = self.p
        self.held[DEPTH + p.y] = value
        for step in (1, 2, 3):
            self.start(
                self.held.at[DEPTH + p.y],
                self.held.at[DEPTH + p.y],
                6 + step,
                6 + step,
                (p.along_y(step), p.slab),
            )

    def sum_y(self):
        p = self.p
        for step in (1, 2, 3):
            self.arrived(
                self.held.at[DEPTH + p.row(-step)], 6 + step, (p.along_y(-step), p.slab)
            )
        value = self.held[DEPTH]
        for place in range(1, BREADTH):
            value = value + self.held[DEPTH + place]
        return value

    def along_slab(self, value):
        p = self.p
        self.shared[p.slab] = value
        for step in range(1, 8):
            self.start(
                self.shared.at[p.slab],
                self.shared.at[p.slab],
                9 + step,
                9 + step,
                (p.coil, (p.slab + step) % 8),
            )

    def sum_slab(self):
        p = self.p
        for step in range(1, 8):
            back = (p.slab - step + 8) % 8
            self.arrived(self.shared.at[back], 9 + step, (p.coil, back))
        value = self.shared[0]
        for place in range(1, 8):
            value = value + self.shared[place]
        return value


def gather_kernel(source, target, *scratch):
    place = Place()
    greet(place, True, 0)
    gather = Gather(place, source, target, *scratch)
    gather.begin()
    gather.spread()
    gather.forward()
    gather.finish()


def exchange_kernel(source, target, *scratch):
    place = Place()
    greet(place, False, 1)
    exchange = Exchange(place, source, target, *scratch)
    exchange.begin()
    exchange.forward()
    exchange.finish()


def back_kernel(blocks, saved, sums, blocks_out, saved_out, sums_out, *scratch):
    place = Place()
    greet(place, True, 2, rows=True)
    exchange = Exchange(place, blocks, blocks_out, *scratch[:3])
    gather = Gather(place, saved, saved_out, *scratch[3:5])
    total = Total(place, *scratch[5:])
    total.along_z(sums[...])
    exchange.begin()
    gather.begin()
    total.along_y(total.sum_z())
    gather.spread()
    exchange.forward()
    total.along_slab(total.sum_y())
    gather.forward()
    sums_out[...] = total.sum_slab()
    exchange.finish()
    gather.finish()
    total.drain()


def whole(value):
    return jnp.sum(jnp.sum(value, axis=1, keepdims=True), axis=0, keepdims=True)


def turn_kernel(
    terms, blocks, direction, sums, blocks_out, residual_out, gathered, held, *scratch
):
    place = Place()
    greet(place, True, 1)
    scatter = Scatter(place, terms, *scratch[:7])
    exchange = Exchange(place, blocks, blocks_out, *scratch[7:10])
    gather = Gather(place, held, gathered, *scratch[10:12])
    scatter.begin()
    exchange.begin()
    scatter.forward()
    exchange.forward()
    scatter.columns()
    norm, energy = whole(sums[0:8]), whole(sums[8:16])
    alpha = norm / (energy + DAMPING * norm)
    current = direction[...]
    image = scatter.total() + DAMPING * current
    residual = current - alpha[None] * image
    residual_out[...] = residual
    held[...] = residual.astype(BF16)
    gather.begin()
    gather.spread()
    gather.forward()
    exchange.finish()
    gather.finish()
    scatter.drain()


def total_kernel(values, values_out, *scratch):
    place = Place()
    greet(place, True, 2, rows=True)
    total = Total(place, *scratch)
    total.along_z(values[...])
    total.along_y(total.sum_z())
    value = total.sum_y()
    values_out[0:32] = value[0:32]
    total.along_slab(value[32:40])
    values_out[32:40] = total.sum_slab()
    total.drain()


def front(maps, image, plane, out):
    cosine, sine = plane[0], plane[1]

    def group(g, carry):
        part = pl.ds(g * 8, 8)
        maps_re, maps_im = maps[part, 0].astype(F32), maps[part, 1].astype(F32)
        image_re, image_im = image[part, 0].astype(F32), image[part, 1].astype(F32)
        real = (maps_re * image_re - maps_im * image_im).astype(BF16).reshape(N, N)
        imag = (maps_re * image_im + maps_im * image_re).astype(BF16).reshape(N, N)
        both = ((1,), (1,))
        rows_re = dot(cosine, real, both) + dot(sine, imag, both)
        rows_im = dot(cosine, imag, both) - dot(sine, real, both)
        out[:, g, 0] = rows_re.astype(BF16).reshape(8, 32, N)
        out[:, g, 1] = rows_im.astype(BF16).reshape(8, 32, N)
        return carry

    lax.fori_loop(0, 4, group, 0)


def spectrum(blocks, plane, wide):
    cosine, sine = plane[0], plane[1]

    def lines(g, part):
        pieces = [blocks[s, g, part] for s in range(8)]
        return jnp.concatenate(
            [
                jnp.concatenate([piece[:, 32 * k : 32 * k + 32] for piece in pieces], axis=1)
                for k in range(8)
            ],
            axis=0,
        )

    def group(g, carry):
        real, imag = lines(g, 0), lines(g, 1)
        wide[pl.ds(g * 8, 8), 0] = (dot(real, cosine) + dot(imag, sine)).reshape(8, 32, N)
        wide[pl.ds(g * 8, 8), 1] = (dot(imag, cosine) - dot(real, sine)).reshape(8, 32, N)
        return carry

    lax.fori_loop(0, 4, group, 0)


def strip(ref, part, at):
    return ref[:, part, at, :].reshape(N, N).astype(BF16)


def across(cosine, sine, real, imag):
    return (
        (dot(cosine, real) + dot(sine, imag)).reshape(NZ, 8, N),
        (dot(cosine, imag) - dot(sine, real)).reshape(NZ, 8, N),
    )


def fold(value):
    return jnp.sum(value[:, :, :128] + value[:, :, 128:], axis=0)


def apply_kernel(blocks, weight, plane, depth, kept, energy, out, wide):
    spectrum(blocks, plane, wide)
    cosine_z, sine_z = depth[0], depth[1]

    def chunk(c, total):
        at = pl.ds(pl.multiple_of(c * 8, 8), 8)
        real, imag = across(cosine_z, sine_z, strip(wide, 0, at), strip(wide, 1, at))
        kept[:, 0, at, :] = real
        kept[:, 1, at, :] = imag
        scale = weight[:, at, :]
        real, imag = scale * real, scale * imag
        total = total + fold(real * real + imag * imag)
        real = (scale * real).astype(BF16).reshape(N, N)
        imag = (scale * imag).astype(BF16).reshape(N, N)
        wide[:, 0, at, :] = (dot(cosine_z, real) - dot(sine_z, imag)).reshape(NZ, 8, N)
        wide[:, 1, at, :] = (dot(cosine_z, imag) + dot(sine_z, real)).reshape(NZ, 8, N)
        return total

    energy[...] = lax.fori_loop(0, 4, chunk, jnp.zeros((8, 128), F32))
    cosine, sine = plane[0], plane[1]

    def group(g, carry):
        part = pl.ds(g * 8, 8)
        real = wide[part, 0].reshape(N, N).astype(BF16)
        imag = wide[part, 1].reshape(N, N).astype(BF16)
        for which, value in (
            (0, dot(real, cosine) - dot(imag, sine)),
            (1, dot(imag, cosine) + dot(real, sine)),
        ):
            value = value.astype(BF16).reshape(8, 32, N)
            for s in range(8):
                out[s, g, which] = jnp.concatenate(
                    [value[k][:, 32 * s : 32 * s + 32] for k in range(8)], axis=1
                )
        return carry

    lax.fori_loop(0, 4, group, 0)


def image_kernel(blocks, maps, saved, plane, terms, saved_blocks):
    cosine, sine = plane[0], plane[1]

    def group(g, carry):
        real, imag = blocks[:, g, 0].reshape(N, N), blocks[:, g, 1].reshape(N, N)
        first = ((0,), (0,))
        image_re = (dot(real, cosine, first) - dot(imag, sine, first)).reshape(8, 32, N)
        image_im = (dot(imag, cosine, first) + dot(real, sine, first)).reshape(8, 32, N)
        part = pl.ds(g * 8, 8)
        maps_re, maps_im = maps[part, 0].astype(F32), maps[part, 1].astype(F32)
        terms[part, 0] = (maps_re * image_re + maps_im * image_im).astype(BF16)
        terms[part, 1] = (maps_re * image_im - maps_im * image_re).astype(BF16)
        return carry

    lax.fori_loop(0, 4, group, 0)
    front(maps, saved, plane, saved_blocks)


def front_kernel(maps, image, plane, out):
    front(maps, image, plane, out)


def close_kernel(
    blocks, saved_blocks, first, weight, data, residual, direction, plane, depth,
    kept, lines, wide, wide_saved,
):
    spectrum(blocks, plane, wide)
    spectrum(saved_blocks, plane, wide_saved)
    cosine_z, sine_z = depth[0], depth[1]
    residual_now, direction_now = residual[...], direction[...]

    def chunk(c, totals):
        at = pl.ds(pl.multiple_of(c * 8, 8), 8)
        real, imag = across(cosine_z, sine_z, strip(wide, 0, at), strip(wide, 1, at))
        kept[:, 0, at, :] = real
        kept[:, 1, at, :] = imag
        saved_re, saved_im = across(
            cosine_z, sine_z, strip(wide_saved, 0, at), strip(wide_saved, 1, at)
        )
        first_re, first_im = first[:, 0, at, :], first[:, 1, at, :]
        scale = weight[:, at, :]
        square = scale * scale
        second, mixed = totals
        second = second + fold(square * (real * real + imag * imag))
        mixed = mixed + fold(square * (real * first_re + imag * first_im))
        target_re = data[:, 0, at, :].astype(F32) - 2.0 * scale * saved_re
        target_im = data[:, 1, at, :].astype(F32) - 2.0 * scale * saved_im
        sampled = jnp.where(scale != 0.0, 1.0, 0.0)
        wide[:, 0, at, :] = sampled * (first_re * target_re + first_im * target_im)
        wide[:, 1, at, :] = sampled * (real * target_re + imag * target_im)
        return second, mixed

    zero = jnp.zeros((8, 128), F32)
    second, mixed = lax.fori_loop(0, 4, chunk, (zero, zero))
    lines[0:32, 0:32] = jnp.sum(wide[:, 0], axis=2)
    lines[0:32, 32:64] = jnp.sum(wide[:, 1], axis=2)
    lines[0:32, 64:128] = jnp.zeros((32, 64), F32)

    def narrow(value):
        value = value.reshape(64, N)
        return jnp.sum(value[:, :128] + value[:, 128:], axis=0, keepdims=True)

    lines[32:33] = jnp.sum(second, axis=0, keepdims=True)
    lines[33:34] = jnp.sum(mixed, axis=0, keepdims=True)
    lines[34:35] = narrow(residual_now * residual_now)
    lines[35:36] = narrow(residual_now * direction_now)
    lines[36:40] = jnp.zeros((4, 128), F32)


def shards(cotangent, saved_solution, coil_maps, kspace, mask_logit, reach):
    plane, depth = tables()
    maps = coil_maps[0]
    data = kspace[0]
    centred = (jnp.arange(N, dtype=jnp.int32) + N // 2) % N
    sampled = (centred[None, None, :] >= (N - reach)[:, :, None]).astype(F32)
    gate = jax.nn.sigmoid(mask_logit)
    weight = sampled * gate[:, :, None]
    direction = cotangent[0]
    blocks = jax.ShapeDtypeStruct((8, 4, 2, 32, N), BF16)
    image = jax.ShapeDtypeStruct((NZ, 2, 32, N), BF16)
    kept = jax.ShapeDtypeStruct((NZ, 2, 32, N), F32)
    wide = pltpu.VMEM((NZ, 2, 32, N), F32)
    square = jnp.sum((direction * direction).reshape(8, 16, 128), axis=1)

    gathered = call(gather_kernel, image, Gather.scratch(), 0, name="gather")(
        direction.astype(BF16)
    )
    sent = call(front_kernel, blocks, name="front")(maps, gathered, plane)
    rows = call(exchange_kernel, blocks, Exchange.scratch(), 1, name="exchange")(sent)
    first, energy, back = call(
        apply_kernel,
        (kept, jax.ShapeDtypeStruct((8, 128), F32), blocks),
        [wide],
        name="apply",
    )(rows, weight, plane, depth)
    sums = jnp.concatenate([square, energy], axis=0)
    returned, saved, sums = call(
        back_kernel,
        (blocks, image, jax.ShapeDtypeStruct((16, 128), F32)),
        Exchange.scratch() + Gather.scratch() + Total.scratch(16, 16),
        2,
        name="back",
    )(back, saved_solution[0].astype(BF16), sums)
    terms, saved_sent = call(image_kernel, (image, blocks), name="image")(
        returned, maps, saved, plane
    )
    slice_wide = jax.ShapeDtypeStruct((2, 32, N), F32)
    saved_rows, residual, gathered = call(
        turn_kernel,
        (blocks, slice_wide, image),
        [pltpu.VMEM((2, 32, N), BF16)]
        + Scatter.scratch()
        + Exchange.scratch()
        + Gather.scratch(),
        3,
        name="turn",
    )(terms.reshape(DEPTH, BREADTH, 2, 32, N), saved_sent, direction, sums)
    sent = call(front_kernel, blocks, name="front")(maps, gathered, plane)
    rows = call(exchange_kernel, blocks, Exchange.scratch(), 4, name="exchange2")(sent)
    second, lines = call(
        close_kernel,
        (kept, jax.ShapeDtypeStruct((40, 128), F32)),
        [wide, wide],
        name="close",
    )(rows, saved_rows, first, weight, data, residual, direction, plane, depth)
    lines = call(
        total_kernel,
        jax.ShapeDtypeStruct((40, 128), F32),
        Total.scratch(40, 8),
        5,
        name="total",
    )(lines)
    norm_now, first_energy = jnp.sum(sums[0:8]), jnp.sum(sums[8:16])
    alpha = norm_now / (first_energy + DAMPING * norm_now)
    scalars = jnp.sum(lines[32:36], axis=1)
    second_energy, mixed_energy, norm_next, crossing = [scalars[k] for k in range(4)]
    beta = norm_next / norm_now
    curvature = (second_energy + beta * (2.0 * mixed_energy + beta * first_energy)) + DAMPING * (
        norm_next + beta * (2.0 * crossing + beta * norm_now)
    )
    later = norm_next / curvature
    early = alpha + later * beta
    image_grad = (DAMPING * (early * direction + later * residual))[None]
    kspace_grad = (weight[:, None] * (early * first + later * second)).astype(BF16)[None]
    logit_grad = gate * (1.0 - gate) * (early * lines[0:32, 0:32] + later * lines[0:32, 32:64])
    return (image_grad, kspace_grad, logit_grad)


def solution(mesh):
    placed = (
        P("coil", None, "slab", None),
        P("coil", None, "slab", None),
        P("coil", None, None, "slab", None),
        P("coil", None, None, "slab", None),
        P(None, "slab"),
        P(None, "slab"),
    )
    return jax.shard_map(
        shards,
        mesh=mesh,
        in_specs=placed,
        out_specs=(
            P("coil", None, "slab", None),
            P("coil", None, None, "slab", None),
            P(None, "slab"),
        ),
        check_vma=False,
    )
```

time: 763 us -> 204 us (0.27)
  blocking collectives: 288 us -> 0 us
  waiting for transfers between devices: 219 us -> 0 us
  Pallas kernels: 0 us -> 179 us
  local copies, waits for them, and re-layouts: 143 us -> 0.64 us
  matrix products: 27.2 us -> 0 us
  starting transfers between devices: 21 us -> 0 us
  other arithmetic: 33.3 us -> 13 us
  between operations: 22.1 us -> 8.09 us
    psum x3 -> x0, blocking collectives: 288 us -> none  [the longest x1 140 us: shards(): lax.psum(jnp.stack([line_terms(first_k), line_terms(second_k)]), 'coil')]
    pallas_call x0 -> x11, Pallas kernels: none -> 179 us  [run(): pl.pallas_call(body, out_shape=out_shape, in_specs=[pl.BlockSpec(memory_s...]
    all_gather x3 -> x0, waiting for transfers between devices: 125 us -> none  [gathered_front(): return front(lax.all_gather(shard, 'coil', axis=0, tiled=True))]
    unnamed x5 -> x0, waiting for transfers between devices: 71 us -> none
    unnamed x30 -> x14, local copies, waits for them, and re-layouts: 61.8 us -> 0.03 us
    all_to_all x8 -> x0, local copies, waits for them, and re-layouts: 51.1 us -> none  [the longest x6 38.1 us: to_kspace(): lax.all_to_all(mixed, 'slab', split_axis=3, concat_axis=2, tiled=True)]
    convert_element_type x4 -> x0, local copies, waits for them, and re-layouts: 28.2 us -> none  [the longest x3 21 us: to_kspace(): mixed = jnp.einsum('nixk,inom->moxk', rows, z_fwd, preferred_element_type...]
    dot_general x9 -> x0, matrix products: 27.2 us -> none  [the longest x3 13.9 us: to_kspace(): jnp.einsum('zink,inoq->zokq', swapped, x_fwd, preferred_element_type=jnp....]
  transfers between devices with their start and end apart: 8 -> 0, of which waited for: 5 -> 0; matrix products, arithmetic and copies ran while one was open for 18% -> 0% of each run, Pallas kernels for 0% -> 0%
where the time goes in v2:
time: 204 us; the launch traced here: 201 us
  Pallas kernels  179 us (88%)
  other arithmetic  13 us (6%)
  between operations  8.09 us (4%)
    pallas_call x11, Pallas kernels, run(): pl.pallas_call(body, out_shape=out_shape, in_specs=[pl.BlockSpec(memory_s...  179 us

profile of v2, /device:TPU:2, one launch (start us, length us, event | category | flops | bytes accessed | tf_op | source)
XLA Modules:
  0.0 200.9 jit_solution(6576738093568523653)
XLA Ops:
  0.6 0.7 broadcast_subtract_fusion
  1.4 0.7 add_divide_fusion
  2.1 1.4 convert_bitcast_fusion.saved
  3.5 1.5 bitcast_convert_fusion
  5.0 1.3 compare_select_fusion.weight
  6.3 25.1 %gather.1.image = bf16[32,2,32,256]{3,2,1,0:T(8,128)(2,1)} custom-call(bf16[2,32,256]{2,1,0:T(8,128)(2,1)} %get-tuple-element.31.source), custom_call_target="tpu_custom_call" | custom-call | tf_op jit(solution)/shard_map/gather/pallas_call | solution.py:46
  31.5 4.0 %front.2.source = bf16[8,4,2,32,256]{4,3,2,1,0:T(8,128)(2,1)} custom-call(bf16[32,2,32,256]{3,2,1,0:T(8,128)(2,1)} %bitcast.18, bf16[32,2,32,256]{3,2,1,0:T(8,128)(2,1)} %gather.1.image, bf16[2,256,256]{2,1,0:T(8,128)(2,1)} %constant.34.clone.plane), custom_call_target="tpu_custom_call" | custom-call | tf_op jit(solution)/shard_map/front/pallas_call | solution.py:46
  35.5 17.1 %exchange.1.blocks = bf16[8,4,2,32,256]{4,3,2,1,0:T(8,128)(2,1)} custom-call(bf16[8,4,2,32,256]{4,3,2,1,0:T(8,128)(2,1)} %front.2.source), custom_call_target="tpu_custom_call" | custom-call | tf_op jit(solution)/shard_map/exchange/pallas_call | solution.py:46
  52.6 9.0 %apply.1 = (f32[32,2,32,256]{3,2,1,0:T(8,128)}, f32[8,128]{1,0:T(8,128)}, bf16[8,4,2,32,256]{4,3,2,1,0:T(8,128)(2,1)}) custom-call(bf16[8,4,2,32,256]{4,3,2,1,0:T(8,128)(2,1)} %exchange.1.blocks, f32[32,32,256]{2,1,0:T(8,128)} %compare_select_fusion.weight, bf16[2,256,256]{2,1,0:T(8,128)(2,1)} %constant.34.clone.plane, bf16[2,256,256]{2,1,0:T(8,128)(2,1)} %constant.35.clone.depth), custom_call_target="tpu_custom_call" | custom-call | tf_op jit(solution)/shard_map/apply/pallas_call | solution.py:46
  61.6 1.3 pad_maximum_fusion.sums
  62.9 24.6 %back.1 = (bf16[8,4,2,32,256]{4,3,2,1,0:T(8,128)(2,1)}, bf16[32,2,32,256]{3,2,1,0:T(8,128)(2,1)}, f32[16,128]{1,0:T(8,128)}) custom-call(bf16[8,4,2,32,256]{4,3,2,1,0:T(8,128)(2,1)} %get-tuple-element.16.blocks, bf16[2,32,256]{2,1,0:T(8,128)(2,1)} %convert_bitcast_fusion.saved, f32[16,128]{1,0:T(8,128)} %pad_maximum_fusion.sums), custom_call_target="tpu_custom_call" | custom-call | tf_op jit(solution)/shard_map/back/pallas_call | solution.py:46
  87.5 0.0 copy-start.6
  87.5 5.9 %image.1 = (bf16[32,2,32,256]{3,2,1,0:T(8,128)(2,1)}, bf16[8,4,2,32,256]{4,3,2,1,0:T(8,128)(2,1)}) custom-call(bf16[8,4,2,32,256]{4,3,2,1,0:T(8,128)(2,1)} %get-tuple-element.19.blocks, bf16[32,2,32,256]{3,2,1,0:T(8,128)(2,1)} %bitcast.19, bf16[32,2,32,256]{3,2,1,0:T(8,128)(2,1)} %get-tuple-element.20.saved, bf16[2,256,256]{2,1,0:T(8,128)(2,1)} %constant.34.clone.plane), custom_call_target="tpu_custom_call" | custom-call | tf_op jit(solution)/shard_map/image/pallas_call | solution.py:46
  93.3 0.0 copy-done.6
  93.3 0.7 slice_reduce_fusion
  95.8 39.9 %turn.1 = (bf16[8,4,2,32,256]{4,3,2,1,0:T(8,128)(2,1)}, f32[2,32,256]{2,1,0:T(8,128)}, bf16[32,2,32,256]{3,2,1,0:T(8,128)(2,1)}) custom-call(bf16[8,4,2,32,256]{4,3,2,1,0:T(8,128)(2,1)} %bitcast.23, bf16[8,4,2,32,256]{4,3,2,1,0:T(8,128)(2,1)} %get-tuple-element.22.blocks, f32[2,32,256]{2,1,0:T(8,128)} %bitcast.21, f32[16,128]{1,0:T(8,128)} %get-tuple-element.18.sums), custom_call_target="tpu_custom_call" | custom-call | tf_op jit(solution)/shard_map/turn/pallas_call | solution.py:46
  135.7 4.0 %front.3.source = bf16[8,4,2,32,256]{4,3,2,1,0:T(8,128)(2,1)} custom-call(bf16[32,2,32,256]{3,2,1,0:T(8,128)(2,1)} %bitcast.20, bf16[32,2,32,256]{3,2,1,0:T(8,128)(2,1)} %get-tuple-element.23.image, bf16[2,256,256]{2,1,0:T(8,128)(2,1)} %constant.34.clone.plane), custom_call_target="tpu_custom_call" | custom-call | tf_op jit(solution)/shard_map/front/pallas_call | solution.py:46
  139.7 18.9 %exchange2.1.blocks = bf16[8,4,2,32,256]{4,3,2,1,0:T(8,128)(2,1)} custom-call(bf16[8,4,2,32,256]{4,3,2,1,0:T(8,128)(2,1)} %front.3.source), custom_call_target="tpu_custom_call" | custom-call | tf_op jit(solution)/shard_map/exchange2/pallas_call | solution.py:46
  158.6 0.0 copy-start
  158.6 0.0 copy-start.1
  158.7 9.8 %close.1 = (f32[32,2,32,256]{3,2,1,0:T(8,128)}, f32[40,128]{1,0:T(8,128)}) custom-call(bf16[8,4,2,32,256]{4,3,2,1,0:T(8,128)(2,1)} %exchange2.1.blocks, bf16[8,4,2,32,256]{4,3,2,1,0:T(8,128)(2,1)} %get-tuple-element.24.saved_blocks, f32[32,2,32,256]{3,2,1,0:T(8,128)} %get-tuple-element.25.first, f32[32,32,256]{2,1,0:T(8,128)} %compare_select_fusion.weight, ...), custom_call_target="tpu_custom_call" | custom-call | tf_op jit(solution)/shard_map/close/pallas_call | solution.py:46
  168.4 21.0 %total.1 = f32[40,128]{1,0:T(8,128)} custom-call(f32[40,128]{1,0:T(8,128)} %get-tuple-element.27.values), custom_call_target="tpu_custom_call" | custom-call | tf_op jit(solution)/shard_map/total/pallas_call | solution.py:46
  189.4 0.8 slice_reduce_fusion.2
  190.2 0.6 fusion.3
  196.3 0.0 copy-done
  196.3 0.0 copy-done.1
  196.3 0.0 copy-start.4
  196.3 0.0 copy-start.5
  196.4 0.0 copy-start.2
  196.4 0.0 copy-start.3
  196.4 3.2 %fusion = bf16[1,32,2,32,256]{4,3,2,1,0:T(8,128)(2,1)} fusion(f32[32,2,32,256]{3,2,1,0:T(8,128)} %get-tuple-element.28, f32[32,2,32,256]{3,2,1,0:T(8,128)S(1)} %copy-done.1, f32[]{:T(128)S(6)} %div.15, f32[]{:T(128)S(6)} %add.63, f32[32,32,256]{2,1,0:T(8,128)S(1)} %copy-done), kind=kLoop, calls=%fused_computation.1 | loop fusion | flops 2621440 | bytes 6291464 | tf_op jit(solution)/shard_map/broadcast_in_dim | solution.py:745
  199.6 0.0 copy-done.4
  199.6 0.0 copy-done.5
  199.6 0.7 fusion.1
  200.3 0.0 copy-done.2
  200.3 0.0 copy-done.3
  200.3 0.6 multiply_bitcast_fusion
  (3 shorter events, 0.0 us)
Async XLA Ops:
  87.5 5.9 %copy-start.6 = (f32[16,128]{1,0:T(8,128)S(1)}, f32[16,128]{1,0:T(8,128)}, u32[]{:S(2)}) copy-start(f32[16,128]{1,0:T(8,128)} %get-tuple-element.18.sums) | copy-start | bytes 24580
  158.6 37.7 %copy-start = (f32[32,32,256]{2,1,0:T(8,128)S(1)}, f32[32,32,256]{2,1,0:T(8,128)}, u32[]{:S(2)}) copy-start(f32[32,32,256]{2,1,0:T(8,128)} %compare_select_fusion.weight) | copy-start | bytes 3145732
  158.6 37.7 %copy-start.1 = (f32[32,2,32,256]{3,2,1,0:T(8,128)S(1)}, f32[32,2,32,256]{3,2,1,0:T(8,128)}, u32[]{:S(2)}) copy-start(f32[32,2,32,256]{3,2,1,0:T(8,128)} %get-tuple-element.25.first) | copy-start | bytes 6291460
  196.3 3.3 %copy-start.4 = (f32[40,128]{1,0:T(8,128)S(1)}, f32[40,128]{1,0:T(8,128)}, u32[]{:S(2)}) copy-start(f32[40,128]{1,0:T(8,128)} %total.1) | copy-start | bytes 61444
  196.3 3.3 %copy-start.5 = (f32[32,32]{1,0:T(8,128)S(1)}, f32[32,32]{1,0:T(8,128)}, u32[]{:S(2)}) copy-start(f32[32,32]{1,0:T(8,128)} %param.12) | copy-start | bytes 12292
  196.4 3.9 %copy-start.2 = (f32[1,2,32,256]{3,2,1,0:T(8,128)S(1)}, f32[1,2,32,256]{3,2,1,0:T(8,128)}, u32[]{:S(2)}) copy-start(f32[1,2,32,256]{3,2,1,0:T(8,128)} %param.8) | copy-start | bytes 196612
  196.4 3.9 %copy-start.3 = (f32[2,32,256]{2,1,0:T(8,128)S(1)}, f32[2,32,256]{2,1,0:T(8,128)}, u32[]{:S(2)}) copy-start(f32[2,32,256]{2,1,0:T(8,128)} %get-tuple-element.26.residual) | copy-start | bytes 196612

commit v3 on v2

v3 whole, which is shorter than its diff:
```python
import jax
import jax.numpy as jnp
import numpy as np
from jax import lax
from jax.experimental import pallas as pl
from jax.experimental.pallas import tpu as pltpu
from jax.sharding import PartitionSpec as P

N = 256
NZ = 32
DAMPING = 0.2
DEPTH = 8
BREADTH = 4
NEAREST = (1, -1, 2, -2, 3, -3, 4)
PAIRS = ((0, 1), (-1, 2), (-2, 3), (-3, 4))
GROUPS = 4
MESH = pl.DeviceIdType.MESH
BF16 = jnp.bfloat16
F32 = jnp.float32


def tables():
    def cosine_sine(length):
        index = np.arange(length)
        phase = (index[:, None] * index[None, :] % length).astype(np.float32) * np.float32(
            2.0 * np.pi / length
        )
        factor = np.float32(1.0 / np.sqrt(length))
        return np.cos(phase) * factor, np.sin(phase) * factor

    plane = np.stack(cosine_sine(N))
    eye = np.eye(8, dtype=np.float32)
    depth = np.stack([np.kron(part, eye) for part in cosine_sine(NZ)])
    return jnp.asarray(plane, BF16), jnp.asarray(depth, BF16)


def dot(left, right, dims=((1,), (0,))):
    return lax.dot_general(left, right, (dims, ((), ())), preferred_element_type=F32)


class Place:
    def __init__(self):
        self.coil = lax.axis_index("coil")
        self.slab = lax.axis_index("slab")
        self.z, self.y = self.coil // BREADTH, self.coil % BREADTH
        self.x, self.core = self.slab // 2, self.slab % 2

    def first(self, step):
        return ((self.z + step + DEPTH) % DEPTH) * BREADTH

    def along_z(self, step):
        return self.first(step) + self.y

    def along_y(self, step):
        return self.z * BREADTH + self.row(step)

    def row(self, step):
        return (self.y + step + BREADTH) % BREADTH

    def along_x(self, step, core):
        return ((self.x + step + 4) % 4) * 2 + core


def greet(place):
    barrier = pltpu.get_barrier_semaphore()
    targets = [(place.along_z(step), place.slab) for step in range(1, DEPTH)]
    targets += [(place.along_y(step), place.slab) for step in range(1, BREADTH)]
    targets += [(place.coil, (place.slab + step) % 8) for step in range(1, 8)]
    for target in targets:
        pl.semaphore_signal(barrier, inc=1, device_id=target, device_id_type=MESH)
    pl.semaphore_wait(barrier, len(targets))


def sender(sends, receives):
    started = []

    def start(source, target, number, arrival, device):
        copy = pltpu.make_async_remote_copy(
            src_ref=source,
            dst_ref=target,
            send_sem=sends.at[number],
            recv_sem=receives.at[arrival],
            device_id=device,
            device_id_type=MESH,
        )
        copy.start()
        started.append(copy)

    def arrived(target, arrival, device):
        pltpu.make_async_remote_copy(
            src_ref=target,
            dst_ref=target,
            send_sem=sends.at[0],
            recv_sem=receives.at[arrival],
            device_id=device,
            device_id_type=MESH,
        ).wait_recv()

    def drain():
        for copy in started:
            copy.wait_send()

    return start, arrived, drain


class Exchange:
    COPIES = 13 * GROUPS

    def __init__(self, place, source, target, relay, sends, receives):
        self.p, self.source, self.target, self.relay = place, source, target, relay
        self.start, self.arrived, self.drain = sender(sends, receives)

    @staticmethod
    def scratch():
        return [
            pltpu.VMEM((GROUPS, 8, 2, 32, N), BF16),
            pltpu.VMEM((GROUPS, 8, 2, 32, N), BF16),
            pltpu.VMEM((GROUPS, 2, 2, 32, N), BF16),
            pltpu.SemaphoreType.DMA((Exchange.COPIES,)),
            pltpu.SemaphoreType.DMA((Exchange.COPIES,)),
        ]

    def begin(self, k):
        p, base = self.p, 13 * k
        for way, step in ((0, 1), (1, -1)):
            for core in (0, 1):
                self.start(
                    self.source.at[k, p.along_x(2, core), way],
                    self.relay.at[k, way, core],
                    base + way * 2 + core,
                    base + way * 2 + core,
                    (p.coil, p.along_x(step, p.core)),
                )
        for way, step in ((0, 1), (1, -1)):
            for core in (0, 1):
                self.start(
                    self.source.at[k, p.along_x(step, core)],
                    self.target.at[k, p.slab],
                    base + 4 + way * 2 + core,
                    base + 4 + way * 2 + p.core,
                    (p.coil, p.along_x(step, core)),
                )
        partner = p.along_x(0, 1 - p.core)
        self.start(
            self.source.at[k, partner],
            self.target.at[k, p.slab],
            base + 12,
            base + 12,
            (p.coil, partner),
        )
        self.target[k, p.slab] = self.source[k, p.slab]

    def forward(self, k):
        p, base = self.p, 13 * k
        for way, step in ((0, 1), (1, -1)):
            for core in (0, 1):
                self.arrived(
                    self.relay.at[k, way, core],
                    base + way * 2 + core,
                    (p.coil, p.along_x(-step, p.core)),
                )
                self.start(
                    self.relay.at[k, way, core],
                    self.target.at[k, p.along_x(-step, p.core), way],
                    base + 8 + way * 2 + core,
                    base + 8 + way * 2 + p.core,
                    (p.coil, p.along_x(step, core)),
                )

    def finish(self, k):
        p, base = self.p, 13 * k
        partner = p.along_x(0, 1 - p.core)
        self.arrived(self.target.at[k, partner], base + 12, (p.coil, partner))
        for way, step in ((0, 1), (1, -1)):
            for core in (0, 1):
                near = p.along_x(-step, core)
                self.arrived(self.target.at[k, near], base + 4 + way * 2 + core, (p.coil, near))
        for way, step in ((0, 1), (1, -1)):
            for core in (0, 1):
                far = p.along_x(2, core)
                self.arrived(
                    self.target.at[k, far, way], base + 8 + way * 2 + core, (p.coil, far)
                )


class Gather:
    COPIES = 39

    def __init__(self, place, source, target, sends, receives):
        self.p, self.source, self.target = place, source, target
        self.start, self.arrived, self.drain = sender(sends, receives)

    @staticmethod
    def scratch():
        return [
            pltpu.VMEM((2, 32, N), BF16),
            pltpu.VMEM((GROUPS, 2, BREADTH, 2, 32, N), BF16),
            pltpu.SemaphoreType.DMA((Gather.COPIES,)),
            pltpu.SemaphoreType.DMA((Gather.COPIES,)),
        ]

    @staticmethod
    def held(step):
        return next((k, pair.index(step)) for k, pair in enumerate(PAIRS) if step in pair)

    def pass_on(self, k, spot, source):
        p = self.p
        for way, step in ((0, 1), (1, -1)):
            number = 7 + (k * 2 + spot) * 2 + way
            self.start(
                source, self.target.at[k, spot, p.y], number, number, (p.along_y(step), p.slab)
            )

    def begin(self):
        p = self.p
        self.pass_on(0, 0, self.source)
        for order, step in enumerate(NEAREST):
            k, spot = self.held(step)
            self.start(
                self.source, self.target.at[k, spot, p.y], order, order, (p.along_z(-step), p.slab)
            )
        self.target[0, 0, p.y] = self.source[...]

    def spread(self, k):
        p = self.p
        for spot, step in enumerate(PAIRS[k]):
            if step != 0:
                slot = self.target.at[k, spot, p.y]
                self.arrived(slot, NEAREST.index(step), (p.along_z(step), p.slab))
                self.pass_on(k, spot, slot)

    def forward(self, k):
        p = self.p
        for spot in (0, 1):
            for way, step in ((0, 1), (1, -1)):
                order = (k * 2 + spot) * 2 + way
                slot = self.target.at[k, spot, p.row(-step)]
                self.arrived(slot, 7 + order, (p.along_y(-step), p.slab))
                half = self.target.at[k, spot, p.row(-step), way]
                self.start(half, half, 23 + order, 23 + order, (p.along_y(step), p.slab))

    def finish(self, k):
        p = self.p
        for spot in (0, 1):
            for way, step in ((0, 1), (1, -1)):
                order = (k * 2 + spot) * 2 + way
                self.arrived(
                    self.target.at[k, spot, p.row(2), way],
                    23 + order,
                    (p.along_y(-step), p.slab),
                )


class Scatter:
    COPIES = 6 * GROUPS + 7

    def __init__(self, place, terms, far, near, mixed, rows, column, sends, receives):
        self.p, self.terms = place, terms
        self.far, self.near, self.mixed, self.rows, self.column = far, near, mixed, rows, column
        self.start, self.arrived, self.drain = sender(sends, receives)

    @staticmethod
    def scratch():
        return [
            pltpu.VMEM((GROUPS, 2, BREADTH, 2, 32, N), BF16),
            pltpu.VMEM((GROUPS, 2, 2, 32, N), BF16),
            pltpu.VMEM((GROUPS, 2, 2, 2, 32, N), BF16),
            pltpu.VMEM((GROUPS, 2, 2, 32, N), BF16),
            pltpu.VMEM((GROUPS, 2, 2, 32, N), BF16),
            pltpu.VMEM((DEPTH - 1, 2, 32, N), BF16),
            pltpu.SemaphoreType.DMA((Scatter.COPIES,)),
            pltpu.SemaphoreType.DMA((Scatter.COPIES,)),
        ]

    def begin(self, k):
        p, base = self.p, 6 * k
        for way, step in ((0, 1), (1, -1)):
            self.start(
                self.terms.at[k, :, p.row(2), way],
                self.far.at[k, way],
                base + way,
                base + way,
                (p.along_y(step), p.slab),
            )
        for way, step in ((0, 1), (1, -1)):
            self.start(
                self.terms.at[k, :, p.row(step), 1 - way],
                self.near.at[k, way, 1 - way],
                base + 2 + way,
                base + 2 + way,
                (p.along_y(step), p.slab),
            )

    def forward(self, k):
        p, base = self.p, 6 * k
        for way, step in ((0, 1), (1, -1)):
            self.arrived(self.far.at[k, way], base + way, (p.along_y(-step), p.slab))
            self.mixed[k, way] = (
                self.far[k, way].astype(F32) + self.terms[k, :, p.row(step), way].astype(F32)
            ).astype(BF16)
            self.start(
                self.mixed.at[k, way],
                self.near.at[k, way, way],
                base + 4 + way,
                base + 4 + way,
                (p.along_y(step), p.slab),
            )

    def columns(self, k):
        p, base = self.p, 6 * k
        for way, step in ((0, 1), (1, -1)):
            beside = (p.along_y(-step), p.slab)
            self.arrived(self.near.at[k, way, 1 - way], base + 2 + way, beside)
            self.arrived(self.near.at[k, way, way], base + 4 + way, beside)
        for spot, step in enumerate(PAIRS[k]):
            for part in (0, 1):
                self.rows[k, spot, part] = (
                    self.terms[k, spot, p.y, part].astype(F32)
                    + self.near[k, 0, part, spot].astype(F32)
                    + self.near[k, 1, part, spot].astype(F32)
                ).astype(BF16)
            if step != 0:
                order = NEAREST.index(step)
                self.start(
                    self.rows.at[k, spot],
                    self.column.at[order],
                    6 * GROUPS + order,
                    6 * GROUPS + order,
                    (p.along_z(step), p.slab),
                )

    def total(self):
        p = self.p
        value = self.rows[0, 0].astype(F32)
        for order, step in enumerate(NEAREST):
            self.arrived(
                self.column.at[order], 6 * GROUPS + order, (p.along_z(-step), p.slab)
            )
            value = value + self.column[order].astype(F32)
        return value


class Total:
    COPIES = 17

    def __init__(self, place, held, shared, sends, receives):
        self.p, self.held, self.shared = place, held, shared
        self.start, self.arrived, self.drain = sender(sends, receives)

    @staticmethod
    def scratch(height, shared):
        return [
            pltpu.VMEM((12, height, 128), F32),
            pltpu.VMEM((8, shared, 128), F32),
            pltpu.SemaphoreType.DMA((Total.COPIES,)),
            pltpu.SemaphoreType.DMA((Total.COPIES,)),
        ]

    def along_z(self, value):
        p = self.p
        self.held[p.z] = value
        for order, step in enumerate(NEAREST):
            self.start(
                self.held.at[p.z], self.held.at[p.z], order, order, (p.along_z(step), p.slab)
            )

    def sum_z(self):
        p = self.p
        for order, step in enumerate(NEAREST):
            self.arrived(
                self.held.at[(p.z - step + DEPTH) % DEPTH], order, (p.along_z(-step), p.slab)
            )
        value = self.held[0]
        for place in range(1, DEPTH):
            value = value + self.held[place]
        return value

    def along_y(self, value):
        p = self.p
        self.held[DEPTH + p.y] = value
        for step in (1, 2, 3):
            self.start(
                self.held.at[DEPTH + p.y],
                self.held.at[DEPTH + p.y],
                6 + step,
                6 + step,
                (p.along_y(step), p.slab),
            )

    def sum_y(self):
        p = self.p
        for step in (1, 2, 3):
            self.arrived(
                self.held.at[DEPTH + p.row(-step)], 6 + step, (p.along_y(-step), p.slab)
            )
        value = self.held[DEPTH]
        for place in range(1, BREADTH):
            value = value + self.held[DEPTH + place]
        return value

    def along_slab(self, value):
        p = self.p
        self.shared[p.slab] = value
        for step in range(1, 8):
            self.start(
                self.shared.at[p.slab],
                self.shared.at[p.slab],
                9 + step,
                9 + step,
                (p.coil, (p.slab + step) % 8),
            )

    def sum_slab(self):
        p = self.p
        for step in range(1, 8):
            back = (p.slab - step + 8) % 8
            self.arrived(self.shared.at[back], 9 + step, (p.coil, back))
        value = self.shared[0]
        for place in range(1, 8):
            value = value + self.shared[place]
        return value


def region(place, body):
    def once(turn, carry):
        body()
        return carry

    lax.fori_loop(0, 1 + place.coil // 32, once, 0)


def whole(value):
    return jnp.sum(jnp.sum(value, axis=1, keepdims=True), axis=0, keepdims=True)


def front(place, k, maps, image, plane, out):
    cosine, sine = plane[0], plane[1]
    reals, imags = [], []
    for spot, step in enumerate(PAIRS[k]):
        part = pl.ds(place.first(step), BREADTH)
        maps_re, maps_im = maps[0, part, 0].astype(F32), maps[0, part, 1].astype(F32)
        image_re = image[k, spot, :, 0].astype(F32)
        image_im = image[k, spot, :, 1].astype(F32)
        reals.append((maps_re * image_re - maps_im * image_im).astype(BF16).reshape(128, N))
        imags.append((maps_re * image_im + maps_im * image_re).astype(BF16).reshape(128, N))
    real, imag = jnp.concatenate(reals, axis=0), jnp.concatenate(imags, axis=0)
    both = ((1,), (1,))
    rows_re = dot(cosine, real, both) + dot(sine, imag, both)
    rows_im = dot(cosine, imag, both) - dot(sine, real, both)
    out[k, :, 0] = rows_re.astype(BF16).reshape(8, 32, N)
    out[k, :, 1] = rows_im.astype(BF16).reshape(8, 32, N)


def readouts(place, k, blocks, plane, wide):
    cosine, sine = plane[0], plane[1]

    def lines(part):
        pieces = [blocks[k, s, part] for s in range(8)]
        return jnp.concatenate(
            [
                jnp.concatenate([piece[:, 32 * j : 32 * j + 32] for piece in pieces], axis=1)
                for j in range(8)
            ],
            axis=0,
        )

    real, imag = lines(0), lines(1)
    out_re = (dot(real, cosine) + dot(imag, sine)).reshape(2, BREADTH, 32, N)
    out_im = (dot(imag, cosine) - dot(real, sine)).reshape(2, BREADTH, 32, N)
    for spot, step in enumerate(PAIRS[k]):
        part = pl.ds(place.first(step), BREADTH)
        wide[part, 0] = out_re[spot]
        wide[part, 1] = out_im[spot]


def unread(place, k, wide, plane, out):
    cosine, sine = plane[0], plane[1]

    def lines(which):
        return jnp.concatenate(
            [
                wide[pl.ds(place.first(step), BREADTH), which].reshape(128, N).astype(BF16)
                for step in PAIRS[k]
            ],
            axis=0,
        )

    real, imag = lines(0), lines(1)
    for which, value in (
        (0, dot(real, cosine) - dot(imag, sine)),
        (1, dot(imag, cosine) + dot(real, sine)),
    ):
        value = value.astype(BF16).reshape(8, 32, N)
        for s in range(8):
            out[k, s, which] = jnp.concatenate(
                [value[j][:, 32 * s : 32 * s + 32] for j in range(8)], axis=1
            )


def unfront(place, k, blocks, maps, plane, terms):
    cosine, sine = plane[0], plane[1]
    real, imag = blocks[k, :, 0].reshape(N, N), blocks[k, :, 1].reshape(N, N)
    first = ((0,), (0,))
    image_re = dot(real, cosine, first) - dot(imag, sine, first)
    image_im = dot(imag, cosine, first) + dot(real, sine, first)
    image_re = image_re.reshape(2, BREADTH, 32, N)
    image_im = image_im.reshape(2, BREADTH, 32, N)
    for spot, step in enumerate(PAIRS[k]):
        part = pl.ds(place.first(step), BREADTH)
        maps_re, maps_im = maps[0, part, 0].astype(F32), maps[0, part, 1].astype(F32)
        terms[k, spot, :, 0] = (maps_re * image_re[spot] + maps_im * image_im[spot]).astype(BF16)
        terms[k, spot, :, 1] = (maps_re * image_im[spot] - maps_im * image_re[spot]).astype(BF16)


def strip(ref, part, at):
    return ref[:, part, at, :].reshape(N, N).astype(BF16)


def across(cosine, sine, real, imag):
    return (
        (dot(cosine, real) + dot(sine, imag)).reshape(NZ, 8, N),
        (dot(cosine, imag) - dot(sine, real)).reshape(NZ, 8, N),
    )


def fold(value):
    return jnp.sum(value[:, :, :128] + value[:, :, 128:], axis=0)


def narrow(value):
    value = value.reshape(64, N)
    value = value[:, :128] + value[:, 128:]
    return jnp.sum(value.reshape(8, 8, 128), axis=0)


def strips(body, start):
    return lax.fori_loop(
        0, 4, lambda c, carry: body(pl.ds(pl.multiple_of(c * 8, 8), 8), carry), start
    )


def filtered(wide, weight, depth, kept):
    cosine, sine = depth[0], depth[1]

    def chunk(at, total):
        real, imag = across(cosine, sine, strip(wide, 0, at), strip(wide, 1, at))
        kept[:, 0, at, :] = real
        kept[:, 1, at, :] = imag
        scale = weight[:, at, :]
        real, imag = scale * real, scale * imag
        total = total + fold(real * real + imag * imag)
        real = (scale * real).astype(BF16).reshape(N, N)
        imag = (scale * imag).astype(BF16).reshape(N, N)
        wide[:, 0, at, :] = (dot(cosine, real) - dot(sine, imag)).reshape(NZ, 8, N)
        wide[:, 1, at, :] = (dot(cosine, imag) + dot(sine, real)).reshape(NZ, 8, N)
        return total

    return strips(chunk, jnp.zeros((8, 128), F32))


def closing(wide, wide_saved, first, weight, data, depth, kept):
    cosine, sine = depth[0], depth[1]

    def chunk(at, totals):
        real, imag = across(cosine, sine, strip(wide, 0, at), strip(wide, 1, at))
        kept[:, 0, at, :] = real
        kept[:, 1, at, :] = imag
        saved_re, saved_im = across(
            cosine, sine, strip(wide_saved, 0, at), strip(wide_saved, 1, at)
        )
        first_re, first_im = first[:, 0, at, :], first[:, 1, at, :]
        scale = weight[:, at, :]
        square = scale * scale
        second, mixed = totals
        second = second + fold(square * (real * real + imag * imag))
        mixed = mixed + fold(square * (real * first_re + imag * first_im))
        target_re = data[0, :, 0, at, :].astype(F32) - 2.0 * scale * saved_re
        target_im = data[0, :, 1, at, :].astype(F32) - 2.0 * scale * saved_im
        sampled = jnp.where(scale != 0.0, 1.0, 0.0)
        wide[:, 0, at, :] = sampled * (first_re * target_re + first_im * target_im)
        wide[:, 1, at, :] = sampled * (real * target_re + imag * target_im)
        return second, mixed

    zero = jnp.zeros((8, 128), F32)
    return strips(chunk, (zero, zero))


COUNTS = (4, 4, 4, 5, 5, 5, 5, 8, 4, 4)


def scratch_shapes():
    return (
        Gather.scratch() * 3
        + Exchange.scratch() * 4
        + Scatter.scratch()
        + Total.scratch(16, 16)
        + Total.scratch(40, 8)
        + [pltpu.VMEM((NZ, 2, 32, N), F32)] * 4
    )


def kernel(
    cotangent, saved, maps, data, weight, gain, plane, depth, image_grad, kspace_grad, logit_grad, *scratch
):
    parts, at = [], 0
    for count in COUNTS:
        parts.append(scratch[at : at + count])
        at += count
    wide, wide_saved, first, second = scratch[at:]
    place = Place()
    gather = Gather(place, *parts[0])
    gather_saved = Gather(place, *parts[1])
    gather_next = Gather(place, *parts[2])
    ahead = Exchange(place, *parts[3])
    ahead_saved = Exchange(place, *parts[4])
    back = Exchange(place, *parts[5])
    ahead_next = Exchange(place, *parts[6])
    scatter = Scatter(place, *parts[7])
    early_sums = Total(place, *parts[8])
    late_sums = Total(place, *parts[9])

    direction = cotangent[0]
    gather.source[...] = direction.astype(BF16)
    gather_saved.source[...] = saved[0].astype(BF16)
    norm_part = narrow(direction * direction)
    greet(place)

    def turn_out(g, e, k):
        g.finish(k)
        region(place, lambda: front(place, k, maps, g.target, plane, e.source))
        e.begin(k)

    def arrive(e, k, to):
        e.finish(k)
        region(place, lambda: readouts(place, k, e.target, plane, to))

    gather.begin()
    gather.spread(0)
    gather.spread(1)
    gather.forward(0)
    gather.spread(2)
    gather.forward(1)
    turn_out(gather, ahead, 0)
    gather.spread(3)
    gather.forward(2)
    turn_out(gather, ahead, 1)
    ahead.forward(0)
    gather.forward(3)
    turn_out(gather, ahead, 2)
    ahead.forward(1)
    turn_out(gather, ahead, 3)
    gather_saved.begin()
    ahead.forward(2)
    arrive(ahead, 0, wide)
    ahead.forward(3)
    arrive(ahead, 1, wide)
    arrive(ahead, 2, wide)
    arrive(ahead, 3, wide)
    gather_saved.spread(0)
    gather_saved.spread(1)
    gather_saved.spread(2)
    gather_saved.spread(3)
    energy = filtered(wide, weight, depth, first)

    early_sums.along_z(jnp.concatenate([norm_part, energy], axis=0))
    for k in range(GROUPS):
        region(place, lambda: unread(place, k, wide, plane, back.source))
        back.begin(k)
        gather_saved.forward(k)
    early_sums.along_y(early_sums.sum_z())
    back.forward(0)
    gather_saved.finish(0)
    region(
        place, lambda: front(place, 0, maps, gather_saved.target, plane, ahead_saved.source)
    )
    back.forward(1)
    for k in range(GROUPS):
        back.finish(k)
        region(place, lambda: unfront(place, k, back.target, maps, plane, scatter.terms))
        scatter.begin(k)
        if k + 2 < GROUPS:
            back.forward(k + 2)
        if k >= 1:
            scatter.forward(k - 1)
        if k >= 2:
            scatter.columns(k - 2)
        if k == 1:
            early_sums.along_slab(early_sums.sum_y())
    ahead_saved.begin(0)
    scatter.forward(3)
    scatter.columns(2)
    turn_out(gather_saved, ahead_saved, 1)
    scatter.columns(3)
    turn_out(gather_saved, ahead_saved, 2)
    turn_out(gather_saved, ahead_saved, 3)
    sums = early_sums.sum_slab()
    norm, first_energy = whole(sums[0:8]), whole(sums[8:16])
    alpha = norm / (first_energy + DAMPING * norm)
    direction = cotangent[0]
    residual = direction - alpha[None] * (scatter.total() + DAMPING * direction)
    gather_next.source[...] = residual.astype(BF16)
    image_grad[0] = residual

    gather_next.begin()
    for k in range(GROUPS):
        ahead_saved.forward(k)
    gather_next.spread(0)
    gather_next.spread(1)
    gather_next.forward(0)
    gather_next.spread(2)
    gather_next.forward(1)
    turn_out(gather_next, ahead_next, 0)
    gather_next.spread(3)
    gather_next.forward(2)
    turn_out(gather_next, ahead_next, 1)
    ahead_next.forward(0)
    gather_next.forward(3)
    turn_out(gather_next, ahead_next, 2)
    ahead_next.forward(1)
    turn_out(gather_next, ahead_next, 3)
    arrive(ahead_saved, 0, wide_saved)
    ahead_next.forward(2)
    arrive(ahead_saved, 1, wide_saved)
    ahead_next.forward(3)
    arrive(ahead_saved, 2, wide_saved)
    arrive(ahead_saved, 3, wide_saved)
    for k in range(GROUPS):
        arrive(ahead_next, k, wide)
    second_energy, mixed_energy = closing(wide, wide_saved, first, weight, data, depth, second)

    residual = image_grad[0]
    late_sums.along_z(
        jnp.concatenate(
            [
                jnp.concatenate(
                    [
                        jnp.sum(wide[:, 0], axis=2),
                        jnp.sum(wide[:, 1], axis=2),
                        jnp.zeros((NZ, 64), F32),
                    ],
                    axis=1,
                ),
                jnp.sum(second_energy, axis=0, keepdims=True),
                jnp.sum(mixed_energy, axis=0, keepdims=True),
                jnp.sum(narrow(residual * residual), axis=0, keepdims=True),
                jnp.sum(narrow(residual * direction), axis=0, keepdims=True),
                jnp.zeros((4, 128), F32),
            ],
            axis=0,
        )
    )
    late_sums.along_y(late_sums.sum_z())
    lines = late_sums.sum_y()
    late_sums.along_slab(lines[32:40])
    scalars = jnp.sum(late_sums.sum_slab(), axis=1, keepdims=True)
    second_all, mixed_all, norm_next, crossing = [scalars[k : k + 1] for k in range(4)]
    beta = norm_next / norm
    curvature = (second_all + beta * (2.0 * mixed_all + beta * first_energy)) + DAMPING * (
        norm_next + beta * (2.0 * crossing + beta * norm)
    )
    later = norm_next / curvature
    earlier = alpha + later * beta
    image_grad[0] = DAMPING * (earlier[None] * direction + later[None] * residual)
    logit_grad[...] = gain[...] * (earlier * lines[0:32, 0:32] + later * lines[0:32, 32:64])

    def write(at, carry):
        scale = weight[:, at, :]
        for part in (0, 1):
            kept = earlier[None] * first[:, part, at, :] + later[None] * second[:, part, at, :]
            wide[:, part, at, :] = scale * kept
        return carry

    strips(write, 0)
    kspace_grad[0] = wide[...].astype(BF16)
    for part in (
        gather, gather_saved, gather_next, ahead, ahead_saved, back, ahead_next, scatter, early_sums, late_sums
    ):
        part.drain()


def shards(cotangent, saved_solution, coil_maps, kspace, mask_logit, reach):
    plane, depth = tables()
    centred = (jnp.arange(N, dtype=jnp.int32) + N // 2) % N
    sampled = (centred[None, None, :] >= (N - reach)[:, :, None]).astype(F32)
    gate = jax.nn.sigmoid(mask_logit)
    weight = sampled * gate[:, :, None]
    whole_vmem = pl.BlockSpec(memory_space=pltpu.VMEM)
    image_grad, kspace_grad, logit_grad = pl.pallas_call(
        kernel,
        out_shape=(
            jax.ShapeDtypeStruct((1, 2, 32, N), F32),
            jax.ShapeDtypeStruct((1, NZ, 2, 32, N), BF16),
            jax.ShapeDtypeStruct((NZ, 32), F32),
        ),
        in_specs=[whole_vmem] * 8,
        out_specs=[whole_vmem] * 3,
        scratch_shapes=scratch_shapes(),
        compiler_params=pltpu.CompilerParams(
            collective_id=0, has_side_effects=True, vmem_limit_bytes=60 * 1024 * 1024
        ),
        name="pass",
    )(cotangent, saved_solution, coil_maps, kspace, weight, gate * (1.0 - gate), plane, depth)
    return (image_grad, kspace_grad, logit_grad)


def solution(mesh):
    placed = (
        P("coil", None, "slab", None),
        P("coil", None, "slab", None),
        P("coil", None, None, "slab", None),
        P("coil", None, None, "slab", None),
        P(None, "slab"),
        P(None, "slab"),
    )
    return jax.shard_map(
        shards,
        mesh=mesh,
        in_specs=placed,
        out_specs=(
            P("coil", None, "slab", None),
            P("coil", None, None, "slab", None),
            P(None, "slab"),
        ),
        check_vma=False,
    )
```

time: 204 us -> 134 us (0.66)
  Pallas kernels: 179 us -> 124 us
  other arithmetic: 13 us -> 2.66 us
  between operations: 8.09 us -> 0.66 us
  local copies, waits for them, and re-layouts: 0.64 us -> 4.41 us
    pallas_call x11 -> x1, Pallas kernels: 179 us -> 124 us  [shards(): pl.pallas_call(kernel, out_shape=(jax.ShapeDtypeStruct((1, 2, 32, N), F32...]
    unnamed x14 -> x7, local copies, waits for them, and re-layouts: 0.03 us -> 4.41 us
    broadcast_in_dim x2 -> x0, other arithmetic: 3.87 us -> none  [the longest x1 3.23 us: shards(): (weight[:, None] * (early * first + later * second)).astype(BF16)[None]]
    convert_element_type x2 -> x0, other arithmetic: 2.91 us -> none  [the longest x1 1.46 us: shards(): direction.astype(BF16)]
where the time goes in v3:
time: 134 us; the launch traced here: 132 us
  Pallas kernels  124 us (93%)
  local copies, waits for them, and re-layouts  4.41 us (3%)
  other arithmetic  2.66 us (2%)
    pallas_call x1, Pallas kernels, shards(): pl.pallas_call(kernel, out_shape=(jax.ShapeDtypeStruct((1, 2, 32, N), F32...  124 us
    unnamed x7, local copies, waits for them, and re-layouts  4.41 us

profile of v3, /device:TPU:2, one launch (start us, length us, event | category | flops | bytes accessed | tf_op | source)
XLA Modules:
  0.0 131.6 jit_solution(8497236151846151304)
XLA Ops:
  0.6 0.0 copy-start
  0.7 0.7 broadcast_subtract_fusion
  1.4 0.0 copy-done
  1.4 0.6 subtract_multiply_fusion
  2.0 1.3 compare_select_fusion.weight
  3.3 123.9 %pass.1 = (f32[1,2,32,256]{3,2,1,0:T(8,128)}, bf16[1,32,2,32,256]{4,3,2,1,0:T(8,128)(2,1)}, f32[32,32]{1,0:T(8,128)}) custom-call(f32[1,2,32,256]{3,2,1,0:T(8,128)} %cotangent.1, f32[1,2,32,256]{3,2,1,0:T(8,128)} %saved.1, bf16[1,32,2,32,256]{4,3,2,1,0:T(8,128)(2,1)} %maps.1, bf16[1,32,2,32,256]{4,3,2,1,0:T(8,128)(2,1)} %data.1, ...), custom_call_target="tpu_custom_call" | custom-call | tf_op jit(solution)/shard_map/pass/pallas_call | solution.py:788
  127.2 1.5 %copy.14 = f32[1,2,32,256]{3,2,1,0:T(8,128)} copy(f32[1,2,32,256]{3,2,1,0:T(8,128)} %get-tuple-element.8) | data formatting | bytes 131072
  128.7 0.0 copy-start.1
  128.7 2.3 %copy.15 = bf16[1,32,2,32,256]{4,3,2,1,0:T(8,128)(2,1)} copy(bf16[1,32,2,32,256]{4,3,2,1,0:T(8,128)(2,1)} %get-tuple-element.9) | data formatting | bytes 2097152
  131.0 0.0 copy-done.1
  131.0 0.6 copy.16
  (1 shorter events, 0.0 us)
Async XLA Ops:
  0.6 0.7 copy-start
  128.7 2.3 %copy-start.1 = (f32[32,32]{1,0:T(8,128)S(1)}, f32[32,32]{1,0:T(8,128)}, u32[]{:S(2)}) copy-start(f32[32,32]{1,0:T(8,128)} %get-tuple-element.10) | copy-start | bytes 12292
